TPU v7x, 32 devices: a whole 2x2x4 slice. The times are simulated.
32 devices in a mesh: tm: 8 (over z, core), mp: 2 (over y), batch: 2 (over x).
Axes of the slice: x: 2, y: 2, z: 4, core: 2. Of those that a mesh axis runs over, the one named last changes fastest.
Arguments:
- frames: bfloat16 [16384, 1024], P(('batch', 'tm')), parts along dimension 0, may hold values from -40 to 40
- norm_gain: float32 [1024], replicated, may hold values from 0.5 to 1.5
- qkv_weight: bfloat16 [3, 1024, 1024], P(None, None, 'mp'), may hold values from -2 to 2
- out_weight: bfloat16 [1024, 1024], P('mp'), may hold values from -0.1875 to 0.1875
- cotangent: bfloat16 [16384, 1024], P(('batch', 'tm')), parts along dimension 0, may hold values from -6 to 6
- pad_mask: int32 [16384], P('batch'), parts along dimension 0, may hold values from 0 to 1, as said below
- utt_lengths: int32 [16], P('batch'), parts along dimension 0, may hold values from 1 to 2048, 8192 in all
Outputs:
- frame_grad: bfloat16 [16384, 1024], P(('batch', 'tm'), 'mp'), parts along dimension 0
- qkv_grad: float32 [6, 1024, 1024], P('batch', 'tm', 'mp'), parts along dimension 0
- out_grad: float32 [2048, 1024], P(('batch', 'mp'), 'tm'), parts along dimension 0
There are 2 independent parts, one for each index of `batch`. A program takes and returns all parts, laid end to end along the dimension named above; an argument that names none is the same for every part. Nothing has to cross between parts.
Inputs may be any that keep to these rules, and one draw needn't show every extreme that they name: `pad_mask`: in each aligned block of 256 frames, the padding frames form the tail of the block, fewer than 128 of them. `utt_lengths`: 8 lengths that sum to 8192; the largest is exactly 2048.
All inputs are finite; a program needn't handle non-finite values.
Results may differ from a plain program's by a relative error of at most 0.012.
The roundings to bfloat16 on the way count: a program that leaves them out, or rounds other values in their place, can miss the bound.
Values may be sent and summed in bfloat16 or wider, within the bound.
A program may use at most 128 MiB of HBM per device.

v0:
```python
import jax
import jax.numpy as jnp
from jax import lax
from jax.sharding import PartitionSpec as P

HS = 128
CH = 32


EPSILON = 1e-05


def with_halo(block, sides, width):
    for axis, dim in sides:
        count = lax.axis_size(axis)
        forward = [(i, i + 1) for i in range(count - 1)]
        backward = [(target, source) for source, target in forward]
        low = lax.ppermute(
            lax.slice_in_dim(block, block.shape[dim] - width, None, axis=dim), axis, forward
        )
        high = lax.ppermute(lax.slice_in_dim(block, 0, width, axis=dim), axis, backward)
        block = jnp.concatenate([low, block, high], axis=dim)
    return block


def layer_norm(frames, norm_gain):
    values = frames.astype(jnp.float32)
    center = values - jnp.mean(values, axis=-1, keepdims=True)
    inverse = lax.rsqrt(jnp.mean(center * center, axis=-1, keepdims=True) + EPSILON)
    normal_form = center * inverse
    return (normal_form, inverse, (normal_form * norm_gain).astype(jnp.bfloat16))


def norm_backward(incoming, normal_form, inverse, norm_gain):
    scaled = incoming * norm_gain
    mean_grad = jnp.mean(scaled, axis=-1, keepdims=True)
    mean_proj = jnp.mean(scaled * normal_form, axis=-1, keepdims=True)
    return inverse * (scaled - mean_grad - normal_form * mean_proj)


def windows(block_rows):
    block_count = block_rows.shape[0] - 2
    return jnp.concatenate(
        [block_rows[:block_count], block_rows[1 : block_count + 1], block_rows[2:]], axis=1
    )


def fold_keys(window):
    block_width = window.shape[1] // 3
    trailing = [(0, 0)] * (window.ndim - 1)
    pieces = [
        jnp.pad(
            window[:, offset * block_width : (offset + 1) * block_width],
            [(offset, 2 - offset)] + trailing,
        )
        for offset in range(3)
    ]
    return pieces[0] + pieces[1] + pieces[2]


def permitted(query_start, query_count, key_start, key_count, pad_mask, utt_lengths):
    utt_ends = jnp.cumsum(utt_lengths)
    query_pos = query_start + jnp.arange(query_count, dtype=jnp.int32)
    key_pos = key_start + jnp.arange(key_count, dtype=jnp.int32)

    def segment(positions):
        return jnp.sum((utt_ends[None, :] <= positions[:, None]).astype(jnp.int32), axis=1)

    padded = jnp.pad(pad_mask, 2 * CH)
    live_keys = lax.dynamic_slice(
        padded, (jnp.asarray(key_start + 2 * CH, jnp.int32),), (key_count,)
    )
    query_cells = query_pos.reshape(-1, CH)
    query_seg = segment(query_pos).reshape(-1, CH)
    key_cells = windows(key_pos.reshape(-1, CH))
    key_seg = windows(segment(key_pos).reshape(-1, CH))
    key_live = windows(live_keys.reshape(-1, CH))
    same_utt = query_seg[:, :, None] == key_seg[:, None, :]
    return same_utt & (
        (key_live[:, None, :] == 1) | (query_cells[:, :, None] == key_cells[:, None, :])
    )


def attend(queries, grad_rows, key_blocks, value_blocks, allowed):
    score_scale = HS ** (-0.5)
    key_win = windows(key_blocks)
    value_win = windows(value_blocks)
    scores = (
        jnp.einsum("cihd,cjhd->chij", queries, key_win, preferred_element_type=jnp.float32)
        * score_scale
    )
    scores = jnp.where(allowed[:, None], scores, -1e30)
    row_max = jnp.max(scores, axis=-1, keepdims=True)
    weights = jnp.exp(scores - row_max)
    attn_probs = weights / jnp.sum(weights, axis=-1, keepdims=True)
    rounded = attn_probs.astype(jnp.bfloat16)
    mixed_out = jnp.einsum(
        "chij,cjhd->cihd", rounded, value_win, preferred_element_type=jnp.float32
    ).astype(jnp.bfloat16)
    prob_grad = jnp.einsum(
        "cihd,cjhd->chij", grad_rows, value_win, preferred_element_type=jnp.float32
    )
    centre = jnp.sum(attn_probs * prob_grad, axis=-1, keepdims=True)
    score_grad = (attn_probs * (prob_grad - centre) * score_scale).astype(jnp.bfloat16)
    query_grad = jnp.einsum(
        "chij,cjhd->cihd", score_grad, key_win, preferred_element_type=jnp.float32
    )
    key_grad = fold_keys(
        jnp.einsum("chij,cihd->cjhd", score_grad, queries, preferred_element_type=jnp.float32)
    )
    value_grad = fold_keys(
        jnp.einsum("chij,cihd->cjhd", rounded, grad_rows, preferred_element_type=jnp.float32)
    )
    return (mixed_out, query_grad, key_grad, value_grad)


def on_device(frames, norm_gain, qkv_weight, out_weight, cotangent, pad_mask, utt_lengths):
    frame_rows = frames.shape[0]
    head_cols = qkv_weight.shape[2]
    heads_here = head_cols // HS
    first_row = lax.axis_index("tm") * frame_rows
    normal_form, inverse, normed = layer_norm(frames, norm_gain)
    projected = jnp.einsum(
        "rd,mdh->mrh", normed, qkv_weight, preferred_element_type=jnp.float32
    ).astype(jnp.bfloat16)
    live_rows = lax.dynamic_slice(pad_mask, (first_row,), (frame_rows,))
    masked = cotangent * live_rows.astype(jnp.bfloat16)[:, None]
    grad_heads = jnp.dot(masked, out_weight.T, preferred_element_type=jnp.float32).astype(
        jnp.bfloat16
    )

    def blocks(tensor):
        return tensor.reshape(-1, CH, heads_here, HS)

    stacked = jnp.concatenate([projected, grad_heads[None]], axis=0)
    extended = with_halo(stacked, (("tm", 1),), 2 * CH)
    query_rim = extended[:, CH:-CH]
    allowed = permitted(
        first_row - CH,
        frame_rows + 2 * CH,
        first_row - 2 * CH,
        frame_rows + 4 * CH,
        pad_mask,
        utt_lengths,
    )
    mixed_ext, query_ext, key_ext, value_ext = attend(
        blocks(query_rim[0]),
        blocks(query_rim[3]),
        blocks(extended[1]),
        blocks(extended[2]),
        allowed,
    )
    mixed_out = mixed_ext[1:-1]
    query_grad = query_ext[1:-1]
    key_grad = key_ext[2:-2]
    value_grad = value_ext[2:-2]
    all_grads = (
        jnp.stack([query_grad, key_grad, value_grad])
        .reshape(3, frame_rows, head_cols)
        .astype(jnp.bfloat16)
    )
    mixed_rows = mixed_out.reshape(frame_rows, head_cols)
    weight_terms = jnp.einsum("rd,mrh->mdh", normed, all_grads, preferred_element_type=jnp.float32)
    out_terms = jnp.einsum("rh,rd->hd", mixed_rows, masked, preferred_element_type=jnp.float32)
    qkv_grad, out_grad = (
        lax.psum_scatter(weight_terms, "tm", scatter_dimension=1, tiled=True),
        lax.psum_scatter(out_terms, "tm", scatter_dimension=1, tiled=True),
    )
    incoming = jnp.einsum("mrh,mdh->rd", all_grads, qkv_weight, preferred_element_type=jnp.float32)
    head_total = lax.psum(incoming, "mp")
    full_grad = norm_backward(head_total, normal_form, inverse, norm_gain)
    share_cols = full_grad.shape[1] // lax.axis_size("mp")
    frame_grad = lax.dynamic_slice_in_dim(
        full_grad, lax.axis_index("mp") * share_cols, share_cols, 1
    )
    return (frame_grad.astype(jnp.bfloat16), qkv_grad, out_grad)


def solution(mesh):
    placed = (
        P(("batch", "tm"), None),
        P(),
        P(None, None, "mp"),
        P("mp", None),
        P(("batch", "tm"), None),
        P("batch"),
        P("batch"),
    )
    return jax.shard_map(
        on_device,
        mesh=mesh,
        in_specs=placed,
        out_specs=(P(("batch", "tm"), "mp"), P("batch", "tm", "mp"), P(("batch", "mp"), "tm")),
        check_vma=False,
    )
```

profile of v0, /device:TPU:0, one launch (start us, length us, event | category | flops | bytes accessed | tf_op | source)
XLA Modules:
  0.0 311.9 jit_solution(12134649921171048453)
XLA Ops:
  8.1 2.1 convert_reduce_fusion
  10.4 0.7 fusion.4
  11.2 3.3 %fusion.34 = bf16[1,1024,512]{2,1,0:T(8,128)(2,1)S(1)} fusion(bf16[512,1024]{1,0:T(8,128)(2,1)} %param.10, bf16[1024,1024]{1,0:T(8,128)(2,1)} %param.11, bf16[1024]{0:T(1024)(128)(2,1)S(1)} %dynamic-slice_convert_fusion), kind=kOutput, calls=%fused_computation.43 | convolution fusion | flops 1075314688 | bytes 4196352 | tf_op jit(solution)/shard_map/dot_general | solution.py:128
  14.6 4.0 %convert_bitcast_fusion = bf16[3,1024,512]{2,1,0:T(8,128)(2,1)S(1)} fusion(bf16[3,1024,512]{2,1,0:T(8,128)(2,1)S(1)} %copy-done, f32[1024]{0:T(1024)S(1)} %copy-done.22, bf16[1024,1024]{1,0:T(8,128)(2,1)S(1)} %copy-done.3, f32[1024]{0:T(1024)S(1)} %add_rsqrt_fusion, f32[1024]{0:T(1024)S(1)} %broadcast_multiply_fusion.3), kind=kOutput, calls=%fused_computation.9 | convolution fusion | flops 3228041216 | bytes 8400896 | tf_op jit(solution)/shard_map/rd,mdh->mrh/dot_general | solution.py:123
  18.6 0.9 pad_maximum_fusion.12
  19.5 0.9 copy-done.1
  20.4 1.3 collective-permute-start.1
  21.7 3.7 %collective-permute-start = (bf16[4,64,512]{2,1,0:T(8,128)(2,1)}, bf16[4,64,512]{2,1,0:T(8,128)(2,1)}, u32[]{:S(2)}, u32[]{:S(2)}) collective-permute-start(bf16[4,64,512]{2,1,0:T(8,128)(2,1)} %get-tuple-element.30), channel_id=1, source_target_pairs={{0,4},{4,8},{8,12},{12,16},{16,20},{20,24},{24,28},{1,5},{5,9},{9,... | collective-permute-start | bytes 786440 | tf_op jit(solution)/shard_map/ppermute | solution.py:18
  25.5 0.6 add_add_fusion.1
  26.3 0.7 convert_reduce_fusion.2
  27.3 0.7 pad_dynamic-slice_fusion.1
  28.1 0.8 concatenate.49
  28.9 0.7 pad_add_fusion.4
  29.6 0.7 add_compare_fusion
  30.3 1.4 eq.47
  31.7 1.4 or_and_fusion
  33.2 3.2 %pad_maximum_fusion = (bf16[1,1088,512]{2,1,0:T(8,128)(2,1)}, bf16[1,1088,512]{2,1,0:T(8,128)(2,1)}, bf16[1,1088,512]{2,1,0:T(8,128)(2,1)}) fusion(bf16[4,64,512]{2,1,0:T(8,128)(2,1)S(1)} %collective-permute-done.1, bf16[1,1024,512]{2,1,0:T(8,128)(2,1)} %copy-done.4, bf16[3,1024,512]{2,1,0:T(8,128)(2,1)} %copy-done.1, ...), kind=kLoop, calls=%fused_computation.44 | loop fusion | flops 10027008 | bytes 8060928 | tf_op jit(solution)/shard_map/concatenate | solution.py:22
  36.4 3.1 slice.216
  39.5 4.2 %pad_maximum_fusion.11 = (bf16[1,1088,512]{2,1,0:T(8,128)(2,1)}, bf16[1,1088,512]{2,1,0:T(8,128)(2,1)}, bf16[1,1088,512]{2,1,0:T(8,128)(2,1)}, bf16[1,1088,512]{2,1,0:T(8,128)(2,1)}, bf16[1,1088,512]{2,1,0:T(8,128)(2,1)}) fusion(bf16[4,64,512]{2,1,0:T(8,128)(2,1)S(1)} %collective-permute-done.1, bf16[4,64,512]{2,1,0:T(8,128)(2,1)} %collective-permute-done, ...), kind=kLoop, calls=%fused_computation.55 | loop fusion | flops 21168128 | bytes 10289152 | tf_op jit(solution)/shard_map/slice | solution.py:147
  43.7 3.1 reshape_squeeze.8
  46.8 3.1 reshape_squeeze.9
  49.9 3.1 slice.194
  53.0 3.1 slice.214
  56.1 3.1 slice.191
  59.1 3.1 slice.196
  62.2 3.1 slice.212
  65.3 1.6 copy_dynamic-update-slice_fusion.2
  67.2 0.3 copy_dynamic-update-slice_fusion.1
  67.6 0.7 copy-done.10
  68.3 0.4 copy_dynamic-update-slice_fusion
  68.7 3.2 %fusion.47 = f32[34,4,32,96]{3,2,1,0:T(8,128)} fusion(bf16[34,96,4,128]{3,1,2,0:T(8,128)(2,1)S(1)} %copy_dynamic-update-slice_fusion, bf16[34,32,4,128]{3,2,1,0:T(4,128)(2,1)S(1)} %copy-done.8), kind=kOutput, calls=%fused_computation.73 | convolution fusion | flops 106954752 | bytes 6127616 | tf_op jit(solution)/shard_map/cihd,cjhd->chij/dot_general | solution.py:100
  71.9 0.4 copy_dynamic-update-slice_fusion.4
  72.2 0.9 copy-done.12
  73.5 1.8 fusion.50
  75.3 2.2 fusion.69
  77.5 28.3 %fusion.31 = bf16[34,32,4,128]{3,1,2,0:T(8,128)(2,1)} fusion(bf16[34,96,4,128]{3,1,2,0:T(8,128)(2,1)} %copy-done.6, f32[34,4,32,96]{3,2,1,0:T(8,128)} %fusion.47, f32[34,4,32,96]{3,2,1,0:T(8,128)} %get-tuple-element.42, f32[34,4,32]{2,1,0:T(4,128)S(1)} %get-tuple-element.41), kind=kOutput, calls=%fused_computation.42 | convolution fusion | flops 110440800 | bytes 7816192 | tf_op jit(solution)/shard_map/chij,cjhd->cihd/dot_general | solution.py:105
  105.8 31.5 %convolution_bitcast_fusion.1 = f32[34,96,4,128]{3,1,2,0:T(8,128)} fusion(f32[34,4,32,96]{3,2,1,0:T(8,128)} %fusion.47, bf16[34,32,4,128]{3,2,1,0:T(4,128)(2,1)} %reshape_squeeze.8, f32[34,4,32,96]{3,2,1,0:T(8,128)} %get-tuple-element.42, f32[34,4,32]{2,1,0:T(4,128)S(1)} %get-tuple-element.41), kind=kOutput, calls=%fused_computation.11 | convolution fusion | flops 109883744 | bytes 11158528 | tf_op jit(solution)/shard_map/chij,cihd->cjhd/dot_general | solution.py:109
  137.3 13.4 %convolution_bitcast_fusion = f32[34,96,4,128]{3,1,2,0:T(8,128)} fusion(bf16[34,32,4,128]{3,2,1,0:T(4,128)(2,1)} %reshape_squeeze.9, f32[34,4,32]{2,1,0:T(4,128)S(1)} %get-tuple-element.41, f32[34,4,32,96]{3,2,1,0:T(8,128)} %copy-done.5, pred[34,32,96]{2,1,0:T(8,128)(4,1)S(1)} %or_and_fusion), kind=kOutput, calls=%fused_computation.10 | convolution fusion | flops 109048160 | bytes 9591808 | tf_op jit(solution)/shard_map/chij,cihd->cjhd/dot_general | solution.py:112
  150.8 1.2 slice-done
  152.0 1.5 copy.46
  153.5 2.2 stack.12
  155.8 3.8 %fusion.66 = (f32[34,32,4,128]{3,1,2,0:T(8,128)S(1)}, f32[34,32,4,128]{3,1,2,0:T(8,128)S(1)}, f32[34,32,4,128]{3,1,2,0:T(8,128)S(1)}) fusion(f32[34,96,4,128]{3,1,2,0:T(8,128)} %convolution_bitcast_fusion.1), kind=kLoop, calls=%fused_computation.111 | loop fusion | bytes 13369344 | tf_op jit(solution)/shard_map/slice | solution.py:53
  159.5 0.8 fusion.11
  160.3 1.5 copy.48
  161.8 2.3 stack.13
  164.1 2.3 constant_dynamic-update-slice_fusion.2
  166.4 3.8 %fusion.65 = (f32[34,32,4,128]{3,1,2,0:T(8,128)S(1)}, f32[34,32,4,128]{3,1,2,0:T(8,128)S(1)}, f32[34,32,4,128]{3,1,2,0:T(8,128)S(1)}) fusion(f32[34,96,4,128]{3,1,2,0:T(8,128)} %convolution_bitcast_fusion), kind=kLoop, calls=%fused_computation.110 | loop fusion | bytes 13369344 | tf_op jit(solution)/shard_map/slice | solution.py:53
  170.2 0.8 fusion.10
  171.0 1.5 copy.50
  172.5 2.5 stack.14
  174.9 2.4 constant_dynamic-update-slice_fusion.1
  177.3 1.1 constant_dynamic-update-slice_fusion
  178.4 6.9 %convolution_bitcast_fusion.3 = f32[1024,1024]{1,0:T(8,128)} fusion(bf16[3,1024,512]{2,1,0:T(8,128)(2,1)} %constant_dynamic-update-slice_fusion, bf16[3,1024,512]{2,1,0:T(8,128)(2,1)S(1)} %copy-done), kind=kOutput, calls=%fused_computation.18 | convolution fusion | flops 3221225472 | bytes 10485760 | tf_op jit(solution)/shard_map/mrh,mdh->rd/dot_general | solution.py:169
  185.3 0.6 copy-done.19
  186.0 8.8 %convolution_bitcast_fusion.2 = f32[3,1024,512]{1,2,0:T(8,128)} fusion(bf16[3,1024,512]{2,1,0:T(8,128)(2,1)} %constant_dynamic-update-slice_fusion, f32[1024]{0:T(1024)S(1)} %copy-done.23, bf16[1024,1024]{1,0:T(8,128)(2,1)} %param.7, f32[1024]{0:T(1024)S(1)} %add_rsqrt_fusion, f32[1024]{0:T(1024)S(1)} %copy-done.19), kind=kOutput, calls=%fused_computation.12 | convolution fusion | flops 3226468352 | bytes 11546624 | tf_op jit(solution)/shard_map/rd,mrh->mdh/dot_general | solution.py:163
  194.9 11.3 %fusion.30 = bf16[34,32,4,128]{3,1,2,0:T(8,128)(2,1)} fusion(bf16[34,96,4,128]{3,1,2,0:T(8,128)(2,1)} %copy-done.7, f32[34,4,32]{2,1,0:T(4,128)S(1)} %get-tuple-element.41, f32[34,4,32,96]{3,2,1,0:T(8,128)} %copy-done.5, pred[34,32,96]{2,1,0:T(8,128)(4,1)S(1)} %or_and_fusion), kind=kOutput, calls=%fused_computation.41 | convolution fusion | flops 109605216 | bytes 6249472 | tf_op jit(solution)/shard_map/chij,cjhd->cihd/dot_general | solution.py:97
  206.2 1.2 slice-done.1
  207.4 0.5 copy.52
  208.2 2.7 fusion.15
  210.9 84.6 %all-reduce.9.cloned.1.call-done = f32[1024,1024]{1,0:T(8,128)} async-done(((f32[1024,1024]{1,0:T(8,128)}), f32[1024,1024]{1,0:T(8,128)}) %all-reduce.9.cloned.1.call-update) | async-done | bytes 4194320 | tf_op jit(solution)/shard_map/psum | solution.py:170
  295.4 3.9 %fusion.64 = (f32[1024]{0:T(1024)S(1)}, f32[1024]{0:T(1024)S(1)}, f32[1024,1024]{1,0:T(8,128)S(1)}, f32[1024,1024]{1,0:T(8,128)S(1)}) fusion(f32[1024]{0:T(1024)S(1)} %add_rsqrt_fusion, f32[1024]{0:T(1024)S(1)} %copy-done.19, bf16[1024,1024]{1,0:T(8,128)(2,1)} %param.7, f32[1024,1024]{1,0:T(8,128)} %all-reduce.9.cloned.1.call-done, f32[1024]{0:T(1024)S(1)} %copy-done.23), kind=kLoop, calls=%fused_computation.109 | loop fusion | flops 7337984 | bytes 14700544 | tf_op jit(solution)/shard_map/reduce_sum | solution.py:36
  299.3 1.5 fusion.9
  300.8 2.3 copy.53
  303.1 0.9 reduce-scatter.5.cloned.1.call-done
  (76 shorter events, 2.1 us)
Async XLA Ops:
  8.0 6.5 %copy-start = (bf16[3,1024,512]{2,1,0:T(8,128)(2,1)S(1)}, bf16[3,1024,512]{2,1,0:T(8,128)(2,1)}, u32[]{:S(2)}) copy-start(bf16[3,1024,512]{2,1,0:T(8,128)(2,1)} %param.9) | copy-start | bytes 9437188
  8.0 287.4 %all-reduce.9.cloned.1.call-start = ((), (), s32[]{:S(2)}) async-start(), calls=%async_computation.2 | async-start | bytes 8388608 | tf_op jit(solution)/shard_map/psum | solution.py:170
  8.1 2.4 copy-start.2
  8.1 3.1 copy-start.17
  10.4 4.1 %copy-start.18 = (f32[1024]{0:T(1024)}, f32[1024]{0:T(1024)S(1)}, u32[]{:S(2)}) copy-start(f32[1024]{0:T(1024)S(1)} %broadcast_multiply_fusion.3) | copy-start | bytes 12292
  11.2 3.4 %copy-start.20 = (bf16[1024]{0:T(1024)(128)(2,1)}, bf16[1024]{0:T(1024)(128)(2,1)S(1)}, u32[]{:S(2)}) copy-start(bf16[1024]{0:T(1024)(128)(2,1)S(1)} %dynamic-slice_convert_fusion) | copy-start | bytes 6148
  11.2 3.4 %copy-start.3 = (bf16[1024,1024]{1,0:T(8,128)(2,1)S(1)}, bf16[1024,1024]{1,0:T(8,128)(2,1)}, u32[]{:S(2)}) copy-start(bf16[1024,1024]{1,0:T(8,128)(2,1)} %param.7) | copy-start | bytes 6291460
  11.2 3.4 %copy-start.22 = (f32[1024]{0:T(1024)S(1)}, f32[1024]{0:T(1024)}, u32[]{:S(2)}) copy-start(f32[1024]{0:T(1024)} %param.8) | copy-start | bytes 12292
  14.6 4.0 %copy-start.4 = (bf16[1,1024,512]{2,1,0:T(8,128)(2,1)}, bf16[1,1024,512]{2,1,0:T(8,128)(2,1)S(1)}, u32[]{:S(2)}) copy-start(bf16[1,1024,512]{2,1,0:T(8,128)(2,1)S(1)} %fusion.34) | copy-start | bytes 3145732
  18.6 1.8 copy-start.1
  18.6 7.5 %copy-start.24 = (s32[8]{0:T(128)S(1)}, s32[8]{0:T(128)}, u32[]{:S(2)}) copy-start(s32[8]{0:T(128)} %param.13) | copy-start | bytes 100
  20.4 12.7 %collective-permute-start.1 = (bf16[4,64,512]{2,1,0:T(8,128)(2,1)}, bf16[4,64,512]{2,1,0:T(8,128)(2,1)S(1)}, u32[]{:S(2)}, u32[]{:S(2)}) collective-permute-start(bf16[4,64,512]{2,1,0:T(8,128)(2,1)} %get-tuple-element.29), channel_id=1, source_target_pairs={{4,0},{8,4},{12,8},{16,12},{20,16},{24,20},{28,24},{5,1},{9,5},{13... | collective-permute-start | bytes 786440 | tf_op jit(solution)/shard_map/ppermute | solution.py:21
  21.7 11.4 %collective-permute-start = (bf16[4,64,512]{2,1,0:T(8,128)(2,1)}, bf16[4,64,512]{2,1,0:T(8,128)(2,1)}, u32[]{:S(2)}, u32[]{:S(2)}) collective-permute-start(bf16[4,64,512]{2,1,0:T(8,128)(2,1)} %get-tuple-element.30), channel_id=1, source_target_pairs={{0,4},{4,8},{8,12},{12,16},{16,20},{20,24},{24,28},{1,5},{5,9},{9,... | collective-permute-start | bytes 786440 | tf_op jit(solution)/shard_map/ppermute | solution.py:18
  65.3 1.6 copy-start.14
  65.3 1.9 copy-start.13
  67.0 1.3 copy-start.10
  67.2 1.4 copy-start.8
  68.6 3.2 %copy-start.7 = (bf16[34,96,4,128]{3,1,2,0:T(8,128)(2,1)}, bf16[34,96,4,128]{3,1,2,0:T(8,128)(2,1)S(1)}, u32[]{:S(2)}) copy-start(bf16[34,96,4,128]{3,1,2,0:T(8,128)(2,1)S(1)} %copy_dynamic-update-slice_fusion) | copy-start | bytes 10027012
  68.7 3.2 %copy-start.11 = (bf16[34,32,4,128]{3,2,1,0:T(4,128)(2,1)S(1)}, bf16[34,32,4,128]{3,2,1,0:T(4,128)(2,1)}, u32[]{:S(2)}) copy-start(bf16[34,32,4,128]{3,2,1,0:T(4,128)(2,1)} %slice.194) | copy-start | bytes 3342340
  71.9 1.2 copy-start.12
  71.9 1.6 copy-start.9
  73.5 1.8 copy-start.6
  75.3 2.2 copy-start.5
  150.8 1.2 slice-start
  174.9 2.4 copy-start.15
  185.3 0.7 copy-start.19
  185.3 0.7 copy-start.23
  185.3 115.5 %reduce-scatter.3.cloned.1.call-start = ((), (), s32[]{:S(2)}) async-start(), calls=%async_computation.3 | async-start | bytes 7077888 | tf_op jit(solution)/shard_map/reduce_scatter | solution.py:166
  194.8 109.2 %reduce-scatter.5.cloned.1.call-start = ((), (), s32[]{:S(2)}) async-start(), calls=%async_computation.4 | async-start | bytes 2359296 | tf_op jit(solution)/shard_map/reduce_scatter | solution.py:167
  206.2 1.2 slice-start.1
  206.2 2.0 copy-start.16
  206.2 2.0 copy-start.21
Sparse Core Ops, SparseCore 0:
  185.4 109.9 all-reduce.8
Sparse Core Ops, SparseCore 1:
  194.9 71.6 reduce-scatter.2
  269.3 34.6 reduce-scatter.4
where the time goes:
time: 317 us; the launch traced here: 312 us
  matrix products  115 us (36%)
  waiting for transfers between devices  85.6 us (27%)
  local copies, waits for them, and re-layouts  64.9 us (20%)
  other arithmetic  24.6 us (8%)
  between operations  16.3 us (5%)
  starting transfers between devices  5.15 us (2%)
    psum x1, waiting for transfers between devices, on_device(): head_total = lax.psum(incoming, 'mp')  84.6 us
    dot_general x1, matrix products, attend(): jnp.einsum('chij,cihd->cjhd', score_grad, queries, preferred_element_type...  31.5 us
    dot_general x1, matrix products, attend(): jnp.einsum('chij,cjhd->cihd', score_grad, key_win, preferred_element_type...  28.3 us
    dot_general x1, matrix products, attend(): jnp.einsum('chij,cihd->cjhd', rounded, grad_rows, preferred_element_type=...  13.4 us
    unnamed x57, local copies, waits for them, and re-layouts  13.1 us
    dot_general x1, matrix products, attend(): jnp.einsum('chij,cjhd->cihd', rounded, value_win, preferred_element_type=...  11.3 us
    dot_general x1, matrix products, on_device(): jnp.einsum('rd,mrh->mdh', normed, all_grads, preferred_element_type=jnp.f...  8.83 us
    another operation x4, local copies, waits for them, and re-layouts, on_device(): jnp.stack([query_grad, key_grad, value_grad])  8.04 us
  transfers between devices with their start and end apart: 5, of which 2 were waited for; matrix products, arithmetic and copies ran while one was open for 12% of the time, Pallas kernels for 0%

commit v1 on v0

v1 whole, which is shorter than its diff:
```python
import functools

import jax
import jax.numpy as jnp
from jax import lax
from jax.experimental import pallas as pl
from jax.experimental.pallas import tpu as pltpu
from jax.sharding import PartitionSpec as P

HS = 128
CH = 32
HALO = 2 * CH
TILE = 128
EPSILON = 1e-05
VMEM_LIMIT = 60 * 1024 * 1024

BF = jnp.bfloat16
F32 = jnp.float32


def dims(contract_left, contract_right):
    return (((contract_left,), (contract_right,)), ((), ()))


def mm(left, right, contract_left, contract_right):
    return lax.dot_general(
        left, right, dims(contract_left, contract_right), preferred_element_type=F32
    )


def norm_parts(frames):
    values = frames.astype(F32)
    center = values - jnp.mean(values, axis=-1, keepdims=True)
    inverse = lax.rsqrt(jnp.mean(center * center, axis=-1, keepdims=True) + EPSILON)
    return center * inverse, inverse


def project_kernel(x_ref, gain_ref, w_ref, wo_ref, cot_ref, live_ref,
                   normed_ref, masked_ref, q_ref, k_ref, v_ref, g_ref):
    xhat, _ = norm_parts(x_ref[...])
    normed = (xhat * gain_ref[...]).astype(BF)
    normed_ref[...] = normed
    for piece, out in enumerate((q_ref, k_ref, v_ref)):
        out[...] = mm(normed, w_ref[piece], 1, 0).astype(BF)
    masked = jnp.where(live_ref[...] == 1, cot_ref[...].astype(F32), 0.0).astype(BF)
    masked_ref[...] = masked
    g_ref[...] = mm(masked, wo_ref[...], 1, 1).astype(BF)


def project(frames, gain, w, wo, cot, live):
    rows, depth = frames.shape
    cols = w.shape[2]
    step = min(rows, 256)
    row = lambda width: pl.BlockSpec((step, width), lambda i: (i, 0))
    return pl.pallas_call(
        project_kernel,
        name="project",
        grid=(rows // step,),
        in_specs=[
            row(depth),
            pl.BlockSpec((1, depth), lambda i: (0, 0)),
            pl.BlockSpec(w.shape, lambda i: (0, 0, 0)),
            pl.BlockSpec(wo.shape, lambda i: (0, 0)),
            row(depth),
            row(1),
        ],
        out_specs=[row(depth), row(depth)] + [row(cols)] * 4,
        out_shape=[jax.ShapeDtypeStruct((rows, depth), BF)] * 2
        + [jax.ShapeDtypeStruct((rows, cols), BF)] * 4,
        compiler_params=pltpu.CompilerParams(vmem_limit_bytes=VMEM_LIMIT),
        cost_estimate=pl.CostEstimate(
            flops=8 * rows * depth * cols, bytes_accessed=8 * rows * depth, transcendentals=0
        ),
    )(frames, gain, w, wo, cot, live)


def attend_kernel(qseg_ref, kcode_ref, qm, km, vm, gm, qh, kh, vh, gh,
                  o_ref, dq_ref, dk_ref, dv_ref,
                  qe, ke, ve, ge, oe, dqe, dka, dva):
    rows, cols = qm.shape
    edge = TILE + rows
    for ext, main, halo in ((qe, qm, qh), (ke, km, kh), (ve, vm, vh), (ge, gm, gh)):
        ext[0 : TILE - HALO] = jnp.zeros((TILE - HALO, cols), BF)
        ext[TILE - HALO : TILE] = halo[0:HALO]
        ext[TILE:edge] = main[...]
        ext[edge : edge + HALO] = halo[HALO : 2 * HALO]
        ext[edge + HALO : edge + TILE] = jnp.zeros((TILE - HALO, cols), BF)
    dka[...] = jnp.zeros_like(dka)
    dva[...] = jnp.zeros_like(dva)
    scale = HS ** (-0.5)
    a = lax.broadcasted_iota(jnp.int32, (TILE, 2 * TILE), 0) + HALO
    b = lax.broadcasted_iota(jnp.int32, (TILE, 2 * TILE), 1)
    apart = a // CH - b // CH
    band = (apart >= -1) & (apart <= 1)
    diagonal = a == b

    def tile(t, carry):
        k0 = pl.multiple_of(t * TILE, TILE)
        q0 = pl.multiple_of(t * TILE + HALO, HALO)
        allowed = band & (
            diagonal | (qseg_ref[pl.ds(k0, TILE), :] == kcode_ref[t])
        )
        for h in range(cols // HS):
            sl = slice(h * HS, (h + 1) * HS)
            q = qe[pl.ds(q0, TILE), sl]
            g = ge[pl.ds(q0, TILE), sl]
            k = ke[pl.ds(k0, 2 * TILE), sl]
            v = ve[pl.ds(k0, 2 * TILE), sl]
            scores = jnp.where(allowed, mm(q, k, 1, 1) * scale, -1e30)
            weights = jnp.exp(scores - jnp.max(scores, axis=-1, keepdims=True))
            p = weights * (1.0 / jnp.sum(weights, axis=-1, keepdims=True))
            pb = p.astype(BF)
            dp = mm(g, v, 1, 1)
            delta = jnp.sum(p * dp, axis=-1, keepdims=True)
            ds = (p * (dp - delta) * scale).astype(BF)
            oe[pl.ds(q0, TILE), sl] = mm(pb, v, 1, 0).astype(BF)
            dqe[pl.ds(q0, TILE), sl] = mm(ds, k, 1, 0).astype(BF)
            dka[pl.ds(k0, 2 * TILE), sl] += mm(ds, q, 0, 0)
            dva[pl.ds(k0, 2 * TILE), sl] += mm(pb, g, 0, 0)
        return carry

    lax.fori_loop(0, rows // TILE + 1, tile, 0)
    o_ref[...] = oe[TILE:edge]
    dq_ref[...] = dqe[TILE:edge]
    dk_ref[...] = dka[TILE:edge].astype(BF)
    dv_ref[...] = dva[TILE:edge].astype(BF)


def attend(qseg, kcode, main, halo):
    rows, cols = main[0].shape
    ext = rows + 2 * TILE
    vmem = pl.BlockSpec(memory_space=pltpu.VMEM)
    return pl.pallas_call(
        attend_kernel,
        name="attend",
        in_specs=[vmem] * 10,
        out_specs=[vmem] * 4,
        out_shape=[jax.ShapeDtypeStruct((rows, cols), BF)] * 4,
        scratch_shapes=[pltpu.VMEM((ext, cols), BF)] * 6 + [pltpu.VMEM((ext, cols), F32)] * 2,
        compiler_params=pltpu.CompilerParams(vmem_limit_bytes=VMEM_LIMIT),
        cost_estimate=pl.CostEstimate(
            flops=24 * rows * TILE * cols, bytes_accessed=16 * rows * cols,
            transcendentals=rows * cols,
        ),
    )(qseg, kcode, *main, *halo)


def terms_kernel(normed_ref, masked_ref, o_ref, dq_ref, dk_ref, dv_ref, out_ref):
    cols = o_ref.shape[1]
    normed = normed_ref[...].T
    for piece, ref in enumerate((dq_ref, dk_ref, dv_ref)):
        out_ref[:, piece * cols : (piece + 1) * cols] = mm(normed, ref[...], 1, 0).astype(BF)
    out_ref[:, 3 * cols :] = mm(masked_ref[...].T, o_ref[...], 1, 0).astype(BF)


def weight_terms(normed, masked, o, dq, dk, dv):
    rows, depth = normed.shape
    cols = o.shape[1]
    step = 512
    part = pl.BlockSpec((rows, step), lambda i: (0, i))
    full = pl.BlockSpec((rows, cols), lambda i: (0, 0))
    return pl.pallas_call(
        terms_kernel,
        name="weight_terms",
        grid=(depth // step,),
        in_specs=[part, part, full, full, full, full],
        out_specs=pl.BlockSpec((step, 4 * cols), lambda i: (i, 0)),
        out_shape=jax.ShapeDtypeStruct((depth, 4 * cols), BF),
        compiler_params=pltpu.CompilerParams(vmem_limit_bytes=VMEM_LIMIT),
        cost_estimate=pl.CostEstimate(
            flops=8 * rows * depth * cols, bytes_accessed=8 * rows * depth, transcendentals=0
        ),
    )(normed, masked, o, dq, dk, dv)


def back_kernel(x_ref, gain_ref, w_ref, dq_ref, dk_ref, dv_ref, dy_ref, sums_ref):
    xhat, _ = norm_parts(x_ref[...])
    total = mm(dq_ref[...], w_ref[0], 1, 1)
    total += mm(dk_ref[...], w_ref[1], 1, 1)
    total += mm(dv_ref[...], w_ref[2], 1, 1)
    shares, _, width = dy_ref.shape
    for i in range(shares):
        dy_ref[i] = total[:, i * width : (i + 1) * width].astype(BF)
    scaled = total * gain_ref[...]
    first = jnp.sum(scaled, axis=-1, keepdims=True)
    second = jnp.sum(scaled * xhat, axis=-1, keepdims=True)
    lane = lax.broadcasted_iota(jnp.int32, sums_ref.shape, 1)
    sums_ref[...] = jnp.where(lane == 0, first, second)


def back(frames, gain, w, dq, dk, dv, shares):
    rows, depth = frames.shape
    cols = dq.shape[1]
    step = min(rows, 256)
    row = lambda width: pl.BlockSpec((step, width), lambda i: (i, 0))
    return pl.pallas_call(
        back_kernel,
        name="back",
        grid=(rows // step,),
        in_specs=[
            row(depth),
            pl.BlockSpec((1, depth), lambda i: (0, 0)),
            pl.BlockSpec(w.shape, lambda i: (0, 0, 0)),
            row(cols),
            row(cols),
            row(cols),
        ],
        out_specs=[
            pl.BlockSpec((shares, step, depth // shares), lambda i: (0, i, 0)),
            row(2),
        ],
        out_shape=[
            jax.ShapeDtypeStruct((shares, rows, depth // shares), BF),
            jax.ShapeDtypeStruct((rows, 2), F32),
        ],
        compiler_params=pltpu.CompilerParams(vmem_limit_bytes=VMEM_LIMIT),
        cost_estimate=pl.CostEstimate(
            flops=6 * rows * depth * cols, bytes_accessed=6 * rows * depth, transcendentals=0
        ),
    )(frames, gain, w, dq, dk, dv)


def final_kernel(depth, count, me_ref, x_ref, xs_ref, gain_ref, sums_ref, *refs):
    parts, out_ref = refs[:-1], refs[-1]
    values = x_ref[...].astype(F32)
    mean = jnp.mean(values, axis=-1, keepdims=True)
    center = values - mean
    inverse = lax.rsqrt(jnp.mean(center * center, axis=-1, keepdims=True) + EPSILON)
    xhat = (xs_ref[...].astype(F32) - mean) * inverse
    total = parts[0][0].astype(F32)
    for ref in parts[1:]:
        total += ref[0].astype(F32)
    scaled = total * gain_ref[...]
    first = sums_ref[:, 0:1] * (1.0 / depth)
    second = sums_ref[:, 1:2] * (1.0 / depth)
    out_ref[...] = (inverse * (scaled - first - xhat * second)).astype(BF)


def final(me, frames, gain, sums, own, received):
    rows, depth = frames.shape
    shares, _, width = own.shape
    step = min(rows, 256)
    return pl.pallas_call(
        functools.partial(final_kernel, depth, shares),
        name="final",
        grid_spec=pltpu.PrefetchScalarGridSpec(
            num_scalar_prefetch=1,
            grid=(rows // step,),
            in_specs=[
                pl.BlockSpec((step, depth), lambda i, me: (i, 0)),
                pl.BlockSpec((step, width), lambda i, me: (i, me[0])),
                pl.BlockSpec((1, width), lambda i, me: (0, me[0])),
                pl.BlockSpec((step, 2), lambda i, me: (i, 0)),
                pl.BlockSpec((1, step, width), lambda i, me: (me[0], i, 0)),
            ]
            + [pl.BlockSpec((1, step, width), lambda i, me: (0, i, 0))] * len(received),
            out_specs=pl.BlockSpec((step, width), lambda i, me: (i, 0)),
        ),
        out_shape=jax.ShapeDtypeStruct((rows, width), BF),
        compiler_params=pltpu.CompilerParams(vmem_limit_bytes=VMEM_LIMIT),
        cost_estimate=pl.CostEstimate(
            flops=8 * rows * depth, bytes_accessed=6 * rows * depth, transcendentals=0
        ),
    )(me, frames, frames, gain, sums, own, *received)


def neighbour_rows(frames, cot):
    count = lax.axis_size("tm")
    forward = [(i, i + 1) for i in range(count - 1)]
    backward = [(target, source) for source, target in forward]
    rows = frames.shape[0]
    top = jnp.stack([frames[rows - HALO :], cot[rows - HALO :]])
    bottom = jnp.stack([frames[:HALO], cot[:HALO]])
    low = lax.ppermute(top, "tm", forward)
    high = lax.ppermute(bottom, "tm", backward)
    return jnp.concatenate([low[0], high[0]]), jnp.concatenate([low[1], high[1]])


def on_device(frames, norm_gain, qkv_weight, out_weight, cotangent, pad_mask, utt_lengths):
    rows, depth = frames.shape
    cols = qkv_weight.shape[2]
    tm_count = lax.axis_size("tm")
    mp_count = lax.axis_size("mp")
    mp_at = lax.axis_index("mp")
    first_row = lax.axis_index("tm") * rows
    gain = norm_gain[None, :]

    ext = rows + 2 * TILE
    positions = first_row - TILE + jnp.arange(ext, dtype=jnp.int32)
    ends = jnp.cumsum(utt_lengths)
    segment = jnp.sum((ends[:, None] <= positions[None, :]).astype(jnp.int32), axis=0)
    live = lax.dynamic_slice(jnp.pad(pad_mask, TILE), (first_row,), (ext,))
    code = jnp.where(live == 1, segment, -1).reshape(-1, 1, TILE)
    kcode = jnp.concatenate([code[:-1], code[1:]], axis=2)
    qseg = segment[HALO : ext - HALO][:, None]
    live_main = live[TILE : TILE + rows][:, None]
    live_halo = jnp.concatenate(
        [live[TILE - HALO : TILE], live[TILE + rows : TILE + rows + HALO]]
    )[:, None]

    halo_frames, halo_cot = neighbour_rows(frames, cotangent)
    normed, masked, *main = project(
        frames, gain, qkv_weight, out_weight, cotangent, live_main
    )
    _, _, *halo = project(halo_frames, gain, qkv_weight, out_weight, halo_cot, live_halo)
    o, dq, dk, dv = attend(qseg, kcode, main, halo)

    terms = weight_terms(normed, masked, o, dq, dk, dv)
    summed = lax.psum_scatter(terms, "tm", scatter_dimension=0, tiled=True).astype(F32)
    share = depth // tm_count
    qkv_grad = summed[:, : 3 * cols].reshape(share, 3, cols).transpose(1, 0, 2)
    out_grad = summed[:, 3 * cols :].T

    dy, sums = back(frames, gain, qkv_weight, dq, dk, dv, mp_count)
    sums_flat = sums.T
    total = sums_flat
    received = []
    for shift in range(1, mp_count):
        pairs = [(i, (i + shift) % mp_count) for i in range(mp_count)]
        target = (mp_at + shift) % mp_count
        piece = lax.dynamic_slice_in_dim(dy, target, 1, 0)
        received.append(lax.ppermute(piece, "mp", pairs))
        total = total + lax.ppermute(sums_flat, "mp", pairs)
    me = jnp.reshape(mp_at, (1,)).astype(jnp.int32)
    frame_grad = final(me, frames, gain, total.T, dy, received)
    return (frame_grad, qkv_grad, out_grad)


def solution(mesh):
    placed = (
        P(("batch", "tm"), None),
        P(),
        P(None, None, "mp"),
        P("mp", None),
        P(("batch", "tm"), None),
        P("batch"),
        P("batch"),
    )
    return jax.shard_map(
        on_device,
        mesh=mesh,
        in_specs=placed,
        out_specs=(P(("batch", "tm"), "mp"), P("batch", "tm", "mp"), P(("batch", "mp"), "tm")),
        check_vma=False,
    )
```

time: 317 us -> 131 us (0.41); the launches traced: 312 us -> 130 us
  matrix products: 115 us -> 0 us
  Pallas kernels: 0 us -> 60.5 us
  local copies, waits for them, and re-layouts: 64.9 us -> 9.99 us
  waiting for transfers between devices: 85.6 us -> 35.4 us
  other arithmetic: 24.6 us -> 3.51 us
    dot_general x11 -> x0, matrix products: 115 us -> none  [the longest x1 31.5 us: attend(): jnp.einsum('chij,cihd->cjhd', score_grad, queries, preferred_element_type...]
    psum x1 -> x0, waiting for transfers between devices: 84.6 us -> none  [on_device(): head_total = lax.psum(incoming, 'mp')]
    pallas_call x0 -> x6, Pallas kernels: none -> 60.5 us  [the longest x1 23.8 us: attend(): pl.pallas_call(attend_kernel, name='attend', in_specs=[vmem] * 10, out_sp...]
    ppermute x2 -> x4, waiting for transfers between devices: 0.01 us -> 33.2 us  [the longest x1 33.2 us: on_device(): total = total + lax.ppermute(sums_flat, 'mp', pairs)]
    slice x22 -> x8, local copies, waits for them, and re-layouts: 34.6 us -> 1.65 us  [the longest x2 1.39 us: on_device(): qkv_grad = summed[:, :3 * cols].reshape(share, 3, cols).transpose(1, 0, 2)]
    another operation x6 -> x1, local copies, waits for them, and re-layouts: 14.2 us -> 1.13 us  [neighbour_rows(): top = jnp.stack([frames[rows - HALO:], cot[rows - HALO:]])]
    unnamed x57 -> x12, local copies, waits for them, and re-layouts: 13.1 us -> 2.99 us
    reduce_sum x5 -> x1, other arithmetic: 7.4 us -> 0.09 us  [on_device(): jnp.sum((ends[:, None] <= positions[None, :]).astype(jnp.int32), axis=0)]
  transfers between devices with their start and end apart: 5 -> 5, of which waited for: 2 -> 2; matrix products, arithmetic and copies ran while one was open for 12% -> 5% of each run, Pallas kernels for 0% -> 18%
where the time goes in v1:
time: 131 us; the launch traced here: 130 us
  Pallas kernels  60.5 us (46%)
  waiting for transfers between devices  35.4 us (27%)
  between operations  14.2 us (11%)
  local copies, waits for them, and re-layouts  9.99 us (8%)
  starting transfers between devices  6.23 us (5%)
  other arithmetic  3.51 us (3%)
    ppermute x1, waiting for transfers between devices, on_device(): total = total + lax.ppermute(sums_flat, 'mp', pairs)  33.2 us
    pallas_call x1, Pallas kernels, attend(): pl.pallas_call(attend_kernel, name='attend', in_specs=[vmem] * 10, out_sp...  23.8 us
    pallas_call x2, Pallas kernels, project(): pl.pallas_call(project_kernel, name='project', grid=(rows // step,), in_s...  14.2 us
    pallas_call x1, Pallas kernels, weight_terms(): pl.pallas_call(terms_kernel, name='weight_terms', grid=(depth // step,),...  8.89 us
    pallas_call x1, Pallas kernels, back(): pl.pallas_call(back_kernel, name='back', grid=(rows // step,), in_specs=[...  8.34 us
    pallas_call x1, Pallas kernels, final(): pl.pallas_call(functools.partial(final_kernel, depth, shares), name='fina...  5.22 us
    unnamed x12, local copies, waits for them, and re-layouts  2.99 us
  transfers between devices with their start and end apart: 5, of which 2 were waited for; matrix products, arithmetic and copies ran while one was open for 5% of the time, Pallas kernels for 18%

profile of v1, /device:TPU:0, one launch (start us, length us, event | category | flops | bytes accessed | tf_op | source)
XLA Modules:
  0.0 129.8 jit_solution(5954410207989556249)
XLA Ops:
  7.2 0.0 copy-start.4
  7.2 0.0 copy-start.3
  7.2 0.0 reduce-scatter.2.cloned.1.call-start
  7.2 1.1 slice_bitcast_fusion.7
  8.4 2.4 %collective-permute-start = (bf16[2,64,1024]{2,1,0:T(8,128)(2,1)S(1)}, bf16[2,64,1024]{2,1,0:T(8,128)(2,1)S(1)}, u32[]{:S(2)}, u32[]{:S(2)}) collective-permute-start(bf16[2,64,1024]{2,1,0:T(8,128)(2,1)S(1)} %pad_maximum_fusion), channel_id=1, source_target_pairs={{0,4},{4,8},{8,12},{12,16},{16,20},{20,24},{24,28},{1,5},{5,9},{9,... | collective-permute-start | bytes 786440 | tf_op jit(solution)/shard_map/ppermute | solution.py:274
  10.9 1.3 collective-permute-start.1
  12.2 0.0 copy-done.4
  12.2 0.2 reduce-window.8
  12.4 0.1 convert_reduce_fusion
  12.5 0.0 copy-done.3
  12.5 0.1 fusion.1
  12.6 0.1 pad_dynamic-slice_fusion.2
  12.6 1.0 copy.19.live_ref
  13.7 10.1 %project.2 = (bf16[1024,1024]{1,0:T(8,128)(2,1)}, bf16[1024,1024]{1,0:T(8,128)(2,1)}, bf16[1024,512]{1,0:T(8,128)(2,1)}, bf16[1024,512]{1,0:T(8,128)(2,1)}, bf16...) custom-call(bf16[1024,1024]{1,0:T(8,128)(2,1)} %xs_ref.1, f32[1,1024]{1,0:T(1,128)} %bitcast.35, ...), custom_call_target="tpu_custom_call" | custom-call | flops 4294967296 | bytes 8388608 | tf_op jit(solution)/shard_map/project/pallas_call | solution.py:55
  23.8 0.1 pad_dynamic-slice_fusion.1
  23.9 0.6 pad_add_fusion.kcode_ref
  24.5 0.1 add_bitcast_fusion.1
  24.6 0.1 slice.88
  24.7 0.7 copy.20.live_ref
  25.4 1.0 broadcast_in_dim.23.qseg_ref
  26.4 0.0 collective-permute-done
  26.5 0.0 collective-permute-done.1
  26.5 0.7 pad_maximum_fusion.2.x_ref
  27.2 0.7 pad_maximum_fusion.3.cot_ref
  28.0 4.1 %project.3 = (bf16[128,1024]{1,0:T(8,128)(2,1)}, bf16[128,1024]{1,0:T(8,128)(2,1)}, bf16[128,512]{1,0:T(8,128)(2,1)}, bf16[128,512]{1,0:T(8,128)(2,1)}, bf16[128...) custom-call(bf16[128,1024]{1,0:T(8,128)(2,1)} %pad_maximum_fusion.2.x_ref, f32[1,1024]{1,0:T(1,128)} %bitcast.36, ...), custom_call_target="tpu_custom_call" | custom-call | flops 536870912 | bytes 1048576 | tf_op jit(solution)/shard_map/project/pallas_call | solution.py:55
  32.0 23.8 %attend.1 = (bf16[1024,512]{1,0:T(8,128)(2,1)}, bf16[1024,512]{1,0:T(8,128)(2,1)}, bf16[1024,512]{1,0:T(8,128)(2,1)}, bf16[1024,512]{1,0:T(8,128)(2,1)}) custom-call(s32[1152,1]{1,0:T(8,128)} %broadcast_in_dim.23.qseg_ref, s32[9,1,256]{2,1,0:T(1,128)} %pad_add_fusion.kcode_ref, bf16[1024,512]{1,0:T(8,128)(2,1)} %get-tuple-element.19.qm, ...), custom_call_target="tpu_custom_call" | custom-call | flops 1610612736 | bytes 8388608 | tf_op jit(solution)/shard_map/attend/pallas_call | solution.py:133
  55.8 8.9 %weight_terms.1 = bf16[1024,2048]{1,0:T(8,128)(2,1)} custom-call(bf16[1024,1024]{1,0:T(8,128)(2,1)} %get-tuple-element.32.normed_ref, bf16[1024,1024]{1,0:T(8,128)(2,1)} %get-tuple-element.33.masked_ref, bf16[1024,512]{1,0:T(8,128)(2,1)} %get-tuple-element.34.o_ref, bf16[1024,512]{1,0:T(8,128)(2,1)} %get-tuple-element.27.dq_ref, ...), custom_call_target="tpu_custom_call" | custom-call | flops 4294967296 | bytes 8388608 | tf_op jit(solution)/shard_map/weight_terms/pallas_call | solution.py:162
  64.7 0.0 reduce-scatter.2.cloned.1.call-update
  64.8 8.3 %back.1 = (bf16[2,1024,512]{2,1,0:T(8,128)(2,1)}, f32[1024,2]{1,0:T(8,128)}) custom-call(bf16[1024,1024]{1,0:T(8,128)(2,1)} %xs_ref.1, f32[1,1024]{1,0:T(1,128)} %bitcast.37, bf16[3,1024,512]{2,1,0:T(8,128)(2,1)} %w_ref.5, bf16[1024,512]{1,0:T(8,128)(2,1)} %get-tuple-element.27.dq_ref, bf16[1024,512]{1,0:T(8,128)(2,1)} %get-tuple-element.28.dk_ref, ...), custom_call_target="tpu_custom_call" | custom-call | flops 3221225472 | bytes 6291456 | tf_op jit(solution)/shard_map/back/pallas_call | solution.py:196
  73.1 0.0 copy-start.2
  73.1 1.4 %constant_dynamic-slice_fusion = bf16[1,1024,512]{2,1,0:T(8,128)(2,1)S(1)} fusion(bf16[2,1024,512]{2,1,0:T(8,128)(2,1)} %get-tuple-element.31.refs_0_, s32[]{:T(128)S(6)} %select_n.20), kind=kLoop, calls=%fused_computation.24 | loop fusion | bytes 2097156 | tf_op jit(solution)/shard_map/dynamic_slice | solution.py:321
  74.5 2.4 %collective-permute-start.3 = (bf16[1,1024,512]{2,1,0:T(8,128)(2,1)S(1)}, bf16[1,1024,512]{2,1,0:T(8,128)(2,1)S(1)}, u32[]{:S(2)}, u32[]{:S(2)}) collective-permute-start(bf16[1,1024,512]{2,1,0:T(8,128)(2,1)S(1)} %constant_dynamic-slice_fusion), channel_id=1, source_target_pairs={{0,2},{2,0},{1,3},{3,1},{4,6},{6,4},{5,7},{7,5},{8,10},{10,8},{9,1... | collective-permute-start | bytes 3145736 | tf_op jit(solution)/shard_map/ppermute | solution.py:322
  76.9 0.0 copy-done.2
  76.9 0.1 collective-permute-start.2
  77.0 33.2 %collective-permute-done.2 = f32[2,1024]{0,1:T(8,128)S(1)} collective-permute-done((f32[2,1024]{0,1:T(8,128)S(1)}, f32[2,1024]{0,1:T(8,128)S(1)}, u32[]{:S(2)}, u32[]{:S(2)}) %collective-permute-start.2) | collective-permute-done | bytes 8224 | tf_op jit(solution)/shard_map/ppermute | solution.py:323
  110.1 0.9 add_bitcast_fusion.sums_ref
  111.0 0.0 collective-permute-done.3.refs_1_
  111.0 0.0 copy-start.1
  111.0 1.0 copy-done.1
  112.0 5.2 %final.1 = bf16[1024,512]{1,0:T(8,128)(2,1)} custom-call(s32[1]{0:T(128)} %bitcast.me_ref, bf16[1024,1024]{1,0:T(8,128)(2,1)} %xs_ref.1, bf16[1024,1024]{1,0:T(8,128)(2,1)} %xs_ref.1, f32[1,1024]{1,0:T(1,128)} %bitcast.38, f32[1024,2]{1,0:T(8,128)} %add_bitcast_fusion.sums_ref, bf16[2,1024,512]{2,1,0:T(8,128)(2,1)} %get-tuple-element.31.refs_0_, ...), custom_call_target="tpu_custom_call" | custom-call | flops 8388608 | bytes 6291456 | tf_op jit(solution)/shard_map/final/pallas_call | solution.py:243
  117.2 2.2 %reduce-scatter.2.cloned.1.call-done = bf16[128,2048]{1,0:T(8,128)(2,1)} async-done(((bf16[1024,2048]{1,0:T(8,128)(2,1)}), bf16[128,2048]{1,0:T(8,128)(2,1)}) %reduce-scatter.2.cloned.1.call-update) | async-done | bytes 524304 | tf_op jit(solution)/shard_map/reduce_scatter | solution.py:309
  119.4 0.0 copy-start
  119.4 1.1 slice.95
  120.5 0.3 copy.22
  120.8 1.2 copy.23
  122.0 0.0 copy-done
  122.0 0.1 convert_element_type.7
  122.1 0.8 copy.24
  (9 shorter events, 0.1 us)
Async XLA Ops:
  7.2 5.0 %copy-start.4 = (s32[8]{0:T(128)S(1)}, s32[8]{0:T(128)}, u32[]{:S(2)}) copy-start(s32[8]{0:T(128)} %param.13) | copy-start | bytes 100
  7.2 5.3 %copy-start.3 = (s32[8192]{0:T(1024)S(1)}, s32[8192]{0:T(1024)}, u32[]{:S(2)}) copy-start(s32[8192]{0:T(1024)} %param.12) | copy-start | bytes 98308
  7.2 112.2 %reduce-scatter.2.cloned.1.call-start = ((), (), s32[]{:S(2)}) async-start(), calls=%async_computation.1 | async-start | bytes 4718592 | tf_op jit(solution)/shard_map/reduce_scatter | solution.py:309
  8.4 18.0 %collective-permute-start = (bf16[2,64,1024]{2,1,0:T(8,128)(2,1)S(1)}, bf16[2,64,1024]{2,1,0:T(8,128)(2,1)S(1)}, u32[]{:S(2)}, u32[]{:S(2)}) collective-permute-start(bf16[2,64,1024]{2,1,0:T(8,128)(2,1)S(1)} %pad_maximum_fusion), channel_id=1, source_target_pairs={{0,4},{4,8},{8,12},{12,16},{16,20},{20,24},{24,28},{1,5},{5,9},{9,... | collective-permute-start | bytes 786440 | tf_op jit(solution)/shard_map/ppermute | solution.py:274
  10.9 15.6 %collective-permute-start.1 = (bf16[2,64,1024]{2,1,0:T(8,128)(2,1)S(1)}, bf16[2,64,1024]{2,1,0:T(8,128)(2,1)S(1)}, u32[]{:S(2)}, u32[]{:S(2)}) collective-permute-start(bf16[2,64,1024]{2,1,0:T(8,128)(2,1)S(1)} %pad_maximum_fusion.1), channel_id=1, source_target_pairs={{4,0},{8,4},{12,8},{16,12},{20,16},{24,20},{28,24},{5,1},{9,5},{13... | collective-permute-start | bytes 786440 | tf_op jit(solution)/shard_map/ppermute | solution.py:275
  73.1 3.8 %copy-start.2 = (f32[1024,2]{1,0:T(8,128)S(1)}, f32[1024,2]{1,0:T(8,128)}, u32[]{:S(2)}) copy-start(f32[1024,2]{1,0:T(8,128)} %get-tuple-element.30) | copy-start | bytes 24580
  74.5 36.5 %collective-permute-start.3 = (bf16[1,1024,512]{2,1,0:T(8,128)(2,1)S(1)}, bf16[1,1024,512]{2,1,0:T(8,128)(2,1)S(1)}, u32[]{:S(2)}, u32[]{:S(2)}) collective-permute-start(bf16[1,1024,512]{2,1,0:T(8,128)(2,1)S(1)} %constant_dynamic-slice_fusion), channel_id=1, source_target_pairs={{0,2},{2,0},{1,3},{3,1},{4,6},{6,4},{5,7},{7,5},{8,10},{10,8},{9,1... | collective-permute-start | bytes 3145736 | tf_op jit(solution)/shard_map/ppermute | solution.py:322
  76.9 33.3 %collective-permute-start.2 = (f32[2,1024]{0,1:T(8,128)S(1)}, f32[2,1024]{0,1:T(8,128)S(1)}, u32[]{:S(2)}, u32[]{:S(2)}) collective-permute-start(f32[2,1024]{0,1:T(8,128)S(1)} %bitcast.33), channel_id=1, source_target_pairs={{0,2},{2,0},{1,3},{3,1},{4,6},{6,4},{5,7},{7,5},{8,10},{10,8},{9,1... | collective-permute-start | bytes 24584 | tf_op jit(solution)/shard_map/ppermute | solution.py:323
  111.0 1.0 copy-start.1
  119.4 2.6 %copy-start = (bf16[128,2048]{1,0:T(8,128)(2,1)S(1)}, bf16[128,2048]{1,0:T(8,128)(2,1)}, u32[]{:S(2)}) copy-start(bf16[128,2048]{1,0:T(8,128)(2,1)} %reduce-scatter.2.cloned.1.call-done) | copy-start | bytes 1572868
Sparse Core Ops, SparseCore 0:
  64.9 54.4 reduce-scatter.1

commit v2 on v1

v2 whole, which is shorter than its diff:
```python
import functools

import jax
import jax.numpy as jnp
from jax import lax
from jax.experimental import pallas as pl
from jax.experimental.pallas import tpu as pltpu
from jax.sharding import PartitionSpec as P

HS = 128
CH = 32
HALO = 2 * CH
TILE = 128
EPSILON = 1e-05
VMEM_LIMIT = 60 * 1024 * 1024

BF = jnp.bfloat16
F32 = jnp.float32


def dims(contract_left, contract_right):
    return (((contract_left,), (contract_right,)), ((), ()))


def mm(left, right, contract_left, contract_right):
    return lax.dot_general(
        left, right, dims(contract_left, contract_right), preferred_element_type=F32
    )


def norm_parts(frames):
    values = frames.astype(F32)
    center = values - jnp.mean(values, axis=-1, keepdims=True)
    inverse = lax.rsqrt(jnp.mean(center * center, axis=-1, keepdims=True) + EPSILON)
    return center * inverse, inverse


def project_kernel(x_ref, gain_ref, w_ref, wo_ref, cot_ref, live_ref,
                   normed_ref, masked_ref, q_ref, k_ref, v_ref, g_ref):
    xhat, _ = norm_parts(x_ref[...])
    normed = (xhat * gain_ref[...]).astype(BF)
    normed_ref[...] = normed.T
    for piece, out in enumerate((q_ref, k_ref, v_ref)):
        out[...] = mm(normed, w_ref[piece], 1, 0).astype(BF)
    masked = jnp.where(live_ref[...] == 1, cot_ref[...].astype(F32), 0.0).astype(BF)
    masked_ref[...] = masked.T
    g_ref[...] = mm(masked, wo_ref[...], 1, 1).astype(BF)


def project(frames, gain, w, wo, cot, live):
    rows, depth = frames.shape
    cols = w.shape[2]
    step = min(rows, 256)
    row = lambda width: pl.BlockSpec((step, width), lambda i: (i, 0))
    return pl.pallas_call(
        project_kernel,
        name="project",
        grid=(rows // step,),
        in_specs=[
            row(depth),
            pl.BlockSpec((1, depth), lambda i: (0, 0)),
            pl.BlockSpec(w.shape, lambda i: (0, 0, 0)),
            pl.BlockSpec(wo.shape, lambda i: (0, 0)),
            row(depth),
            row(1),
        ],
        out_specs=[pl.BlockSpec((depth, step), lambda i: (0, i))] * 2 + [row(cols)] * 4,
        out_shape=[jax.ShapeDtypeStruct((depth, rows), BF)] * 2
        + [jax.ShapeDtypeStruct((rows, cols), BF)] * 4,
        compiler_params=pltpu.CompilerParams(vmem_limit_bytes=VMEM_LIMIT),
        cost_estimate=pl.CostEstimate(
            flops=8 * rows * depth * cols, bytes_accessed=8 * rows * depth, transcendentals=0
        ),
    )(frames, gain, w, wo, cot, live)


def backward_kernel(tm_count, mp_count, group_cols, block,
                    qseg_ref, kcode_ref, qm, km, vm, gm, qh, kh, vh, gh,
                    normed_t, masked_t, x_ref, gain_ref, w_ref,
                    frame_ref, qkv_ref, out_ref, *scratch):
    scratch = list(scratch)
    qe, ke, ve, ge, oe, dqe, dka, dva, dkb, dvb, stats, centre = scratch[:12]
    own, away, landed, sums_away, sums_landed = scratch[12:17]
    phases = tm_count.bit_length() - 1
    lists = scratch[17 : 17 + phases]
    arrivals = scratch[17 + phases : 17 + 2 * phases]
    (send_sem, recv_sem, share_send, share_recv, sums_send, sums_recv) = scratch[17 + 2 * phases :]
    rows, cols = qm.shape
    depth = x_ref.shape[1]
    share = depth // mp_count
    chunk = depth // tm_count
    groups = cols // group_cols
    edge = TILE + rows
    tm_at = lax.axis_index("tm")
    mp_at = lax.axis_index("mp")
    bits = [(tm_at // (1 << b)) % 2 for b in range(phases)]
    partners = [tm_at + (1 - 2 * bits[b]) * (1 << b) for b in range(phases)]
    mp_targets = [lax.rem(mp_at + shift, mp_count) for shift in range(1, mp_count)]

    barrier = pltpu.get_barrier_semaphore()
    for partner in partners:
        pl.semaphore_signal(barrier, inc=1, device_id={"tm": partner},
                            device_id_type=pl.DeviceIdType.MESH)
    for target in mp_targets:
        pl.semaphore_signal(barrier, inc=1, device_id={"mp": target},
                            device_id_type=pl.DeviceIdType.MESH)
    pl.semaphore_wait(barrier, phases + mp_count - 1)

    for ext, main, halo in ((qe, qm, qh), (ke, km, kh), (ve, vm, vh), (ge, gm, gh)):
        ext[0 : TILE - HALO] = jnp.zeros((TILE - HALO, cols), BF)
        ext[TILE - HALO : TILE] = halo[0:HALO]
        ext[TILE:edge] = main[...]
        ext[edge : edge + HALO] = halo[HALO : 2 * HALO]
        ext[edge + HALO : edge + TILE] = jnp.zeros((TILE - HALO, cols), BF)
    dka[...] = jnp.zeros_like(dka)
    dva[...] = jnp.zeros_like(dva)
    scale = HS ** (-0.5)
    a = lax.broadcasted_iota(jnp.int32, (TILE, 2 * TILE), 0) + HALO
    b = lax.broadcasted_iota(jnp.int32, (TILE, 2 * TILE), 1)
    apart = a // CH - b // CH
    band = (apart >= -1) & (apart <= 1)
    diagonal = a == b

    def attend(group, lo, hi):
        def tile(t, carry):
            k0 = pl.multiple_of(t * TILE, TILE)
            q0 = pl.multiple_of(t * TILE + HALO, HALO)
            allowed = band & (
                diagonal | (qseg_ref[pl.ds(k0, TILE), :] == kcode_ref[t])
            )
            for h in range(group * group_cols // HS, (group + 1) * group_cols // HS):
                sl = slice(h * HS, (h + 1) * HS)
                q = qe[pl.ds(q0, TILE), sl]
                g = ge[pl.ds(q0, TILE), sl]
                k = ke[pl.ds(k0, 2 * TILE), sl]
                v = ve[pl.ds(k0, 2 * TILE), sl]
                scores = jnp.where(allowed, mm(q, k, 1, 1) * scale, -1e30)
                weights = jnp.exp(scores - jnp.max(scores, axis=-1, keepdims=True))
                p = weights * (1.0 / jnp.sum(weights, axis=-1, keepdims=True))
                pb = p.astype(BF)
                dp = mm(g, v, 1, 1)
                delta = jnp.sum(p * dp, axis=-1, keepdims=True)
                ds = (p * (dp - delta) * scale).astype(BF)
                oe[pl.ds(q0, TILE), sl] = mm(pb, v, 1, 0).astype(BF)
                dqe[pl.ds(q0, TILE), sl] = mm(ds, k, 1, 0).astype(BF)
                dka[pl.ds(k0, 2 * TILE), sl] += mm(ds, q, 0, 0)
                dva[pl.ds(k0, 2 * TILE), sl] += mm(pb, g, 0, 0)
            return carry

        lax.fori_loop(lo, hi, tile, 0)

    def close(group):
        sl = slice(group * group_cols, (group + 1) * group_cols)
        dkb[:, sl] = dka[TILE:edge, sl].astype(BF)
        dvb[:, sl] = dva[TILE:edge, sl].astype(BF)

    def copy(unit, b):
        return pltpu.make_async_remote_copy(
            src_ref=lists[b].at[unit, :, 1 - bits[b]],
            dst_ref=arrivals[b].at[unit],
            send_sem=send_sem.at[unit, b],
            recv_sem=recv_sem.at[unit, b],
            device_id={"tm": partners[b]},
            device_id_type=pl.DeviceIdType.MESH,
        )

    copies = {}
    progress = {}
    step = 256

    def terms(unit):
        group, half = unit // 2, unit % 2
        sl = slice(group * group_cols, (group + 1) * group_cols)
        pairs = (
            ((normed_t, dqe[TILE:edge, sl]), (normed_t, dkb[:, sl]))
            if half == 0
            else ((normed_t, dvb[:, sl]), (masked_t, oe[TILE:edge, sl]))
        )
        for at in range(0, depth, step):
            for side, (left, right) in enumerate(pairs):
                part = mm(left[at : at + step], right, 1, 0).astype(BF)
                for r in range(0, step, chunk):
                    owner = (at + r) // chunk
                    lists[0][unit, owner // 2, owner % 2, :,
                             side * group_cols : (side + 1) * group_cols] = part[r : r + chunk]
        copies[unit, 0] = copy(unit, 0)
        copies[unit, 0].start()
        progress[unit] = 0

    def advance(unit):
        b = progress[unit]
        copies[unit, b].wait_recv()
        if b < phases - 1:
            for j in range(tm_count >> (b + 1)):
                kept = lists[b][unit, j, bits[b]].astype(F32) + arrivals[b][unit, j].astype(F32)
                lists[b + 1][unit, j // 2, j % 2] = kept.astype(BF)
            copies[unit, b + 1] = copy(unit, b + 1)
            copies[unit, b + 1].start()
        else:
            kept = lists[b][unit, 0, bits[b]].astype(F32) + arrivals[b][unit, 0].astype(F32)
            group, half = unit // 2, unit % 2
            sl = slice(group * group_cols, (group + 1) * group_cols)
            first, second = kept[:, :group_cols], kept[:, group_cols:]
            if half == 0:
                qkv_ref[0, :, sl] = first
                qkv_ref[1, :, sl] = second
            else:
                qkv_ref[2, :, sl] = first
                out_ref[sl, :] = second.T
        progress[unit] = b + 1

    def moments():
        for r in range(0, rows, block):
            values = x_ref[r : r + block].astype(F32)
            mean = jnp.mean(values, axis=-1, keepdims=True)
            center = values - mean
            inverse = lax.rsqrt(jnp.mean(center * center, axis=-1, keepdims=True) + EPSILON)
            centre[r : r + block, 0:1] = mean
            centre[r : r + block, 1:2] = inverse

    def incoming(target, r):
        lane = pl.multiple_of(target * share, 128)
        span = pl.ds(lane, share)
        total = mm(dqe[TILE + r : TILE + r + block], w_ref[0, span, :], 1, 1)
        total += mm(dkb[r : r + block], w_ref[1, span, :], 1, 1)
        total += mm(dvb[r : r + block], w_ref[2, span, :], 1, 1)
        xhat = (x_ref[r : r + block, span].astype(F32) - centre[r : r + block, 0:1]) * centre[
            r : r + block, 1:2
        ]
        scaled = total * gain_ref[:, span]
        first = jnp.sum(scaled, axis=-1, keepdims=True)
        second = jnp.sum(scaled * xhat, axis=-1, keepdims=True)
        return total, first, second

    shares = {}

    def away_shares():
        for s, target in enumerate(mp_targets):
            for i, r in enumerate(range(0, rows, block)):
                total, first, second = incoming(target, r)
                away[s, r : r + block] = total.astype(BF)
                shares[s, i] = pltpu.make_async_remote_copy(
                    src_ref=away.at[s, pl.ds(r, block)],
                    dst_ref=landed.at[s, pl.ds(r, block)],
                    send_sem=share_send.at[s, i],
                    recv_sem=share_recv.at[s, i],
                    device_id={"mp": target},
                    device_id_type=pl.DeviceIdType.MESH,
                )
                shares[s, i].start()
                if s == 0:
                    stats[r : r + block, 0:1] = first
                    stats[r : r + block, 1:2] = second
                else:
                    stats[r : r + block, 0:1] += first
                    stats[r : r + block, 1:2] += second

    def own_share():
        for r in range(0, rows, block):
            total, first, second = incoming(mp_at, r)
            own[r : r + block] = total
            if mp_count > 1:
                first += stats[r : r + block, 0:1]
                second += stats[r : r + block, 1:2]
            lane = lax.broadcasted_iota(jnp.int32, (block, 128), 1)
            both = jnp.where(lane == 0, first, second)
            sums_away[:, r : r + block] = both.T[0:8]
        for s, target in enumerate(mp_targets):
            shares[s, -1] = pltpu.make_async_remote_copy(
                src_ref=sums_away,
                dst_ref=sums_landed.at[s],
                send_sem=sums_send.at[s],
                recv_sem=sums_recv.at[s],
                device_id={"mp": target},
                device_id_type=pl.DeviceIdType.MESH,
            )
            shares[s, -1].start()

    def norm_rows():
        span = pl.ds(pl.multiple_of(mp_at * share, 128), share)
        for s in range(mp_count - 1):
            shares[s, -1].wait_recv()
        for i, r in enumerate(range(0, rows, block)):
            total = own[r : r + block]
            both = sums_away[:, r : r + block]
            for s in range(mp_count - 1):
                shares[s, i].wait_recv()
                total += landed[s, r : r + block].astype(F32)
                both += sums_landed[s, :, r : r + block]
            both = both.T * (1.0 / depth)
            inverse = centre[r : r + block, 1:2]
            xhat = (x_ref[r : r + block, span].astype(F32) - centre[r : r + block, 0:1]) * inverse
            scaled = total * gain_ref[:, span]
            frame_ref[r : r + block] = (
                inverse * (scaled - both[:, 0:1] - xhat * both[:, 1:2])
            ).astype(BF)

    tiles = rows // TILE + 1
    for group in range(groups - 1):
        if group == 0:
            attend(group, 0, tiles)
        close(group)
        terms(2 * group)
        terms(2 * group + 1)
        advance(2 * group)
        third = tiles // 3
        attend(group + 1, 0, third)
        advance(2 * group + 1)
        attend(group + 1, third, 2 * third)
        if phases > 1:
            advance(2 * group)
        attend(group + 1, 2 * third, tiles)
        if phases > 1:
            advance(2 * group + 1)
    if groups == 1:
        attend(0, 0, tiles)
    close(groups - 1)
    moments()
    away_shares()
    terms(2 * groups - 2)
    terms(2 * groups - 1)
    advance(2 * groups - 2)
    own_share()
    for b in range(phases):
        for unit in range(2 * groups):
            if progress[unit] == b:
                advance(unit)
    norm_rows()
    for unit in range(2 * groups):
        for b in range(phases):
            copies[unit, b].wait_send()
    for item in shares.values():
        item.wait_send()


def backward(qseg, kcode, main, halo, normed_t, masked_t, frames, gain, w, tm_count, mp_count):
    rows, cols = main[0].shape
    depth = frames.shape[1]
    ext = rows + 2 * TILE
    share = depth // mp_count
    chunk = depth // tm_count
    group_cols = min(cols, 2 * HS)
    units = 2 * (cols // group_cols)
    width = 2 * group_cols
    block = min(rows, 256)
    blocks = rows // block
    peers = max(mp_count - 1, 1)
    phases = tm_count.bit_length() - 1
    vmem = pl.BlockSpec(memory_space=pltpu.VMEM)
    dma = pltpu.SemaphoreType.DMA
    return pl.pallas_call(
        functools.partial(backward_kernel, tm_count, mp_count, group_cols, block),
        name="backward",
        in_specs=[vmem] * 15,
        out_specs=[vmem] * 3,
        out_shape=[
            jax.ShapeDtypeStruct((rows, share), BF),
            jax.ShapeDtypeStruct((3, chunk, cols), F32),
            jax.ShapeDtypeStruct((cols, chunk), F32),
        ],
        scratch_shapes=[pltpu.VMEM((ext, cols), BF)] * 6
        + [pltpu.VMEM((ext, cols), F32)] * 2
        + [pltpu.VMEM((rows, cols), BF)] * 2
        + [pltpu.VMEM((rows, 2), F32)] * 2
        + [
            pltpu.VMEM((rows, share), F32),
            pltpu.VMEM((peers, rows, share), BF),
            pltpu.VMEM((peers, rows, share), BF),
            pltpu.VMEM((8, rows), F32),
            pltpu.VMEM((peers, 8, rows), F32),
        ]
        + [
            pltpu.VMEM((units, tm_count >> (b + 1), 2, chunk, width), BF) for b in range(phases)
        ]
        + [pltpu.VMEM((units, tm_count >> (b + 1), chunk, width), BF) for b in range(phases)]
        + [
            dma((units, phases)),
            dma((units, phases)),
            dma((peers, blocks)),
            dma((peers, blocks)),
            dma((peers,)),
            dma((peers,)),
        ],
        compiler_params=pltpu.CompilerParams(
            vmem_limit_bytes=VMEM_LIMIT, collective_id=0, has_side_effects=True
        ),
        cost_estimate=pl.CostEstimate(
            flops=24 * rows * depth * cols, bytes_accessed=30 * rows * depth,
            transcendentals=rows * cols,
        ),
    )(qseg, kcode, *main, *halo, normed_t, masked_t, frames, gain, w)


def neighbour_rows(frames, cot):
    count = lax.axis_size("tm")
    forward = [(i, i + 1) for i in range(count - 1)]
    backward = [(target, source) for source, target in forward]
    rows = frames.shape[0]
    top = jnp.stack([frames[rows - HALO :], cot[rows - HALO :]])
    bottom = jnp.stack([frames[:HALO], cot[:HALO]])
    low = lax.ppermute(top, "tm", forward)
    high = lax.ppermute(bottom, "tm", backward)
    return jnp.concatenate([low[0], high[0]]), jnp.concatenate([low[1], high[1]])


def on_device(frames, norm_gain, qkv_weight, out_weight, cotangent, pad_mask, utt_lengths):
    rows = frames.shape[0]
    tm_count = lax.axis_size("tm")
    mp_count = lax.axis_size("mp")
    first_row = lax.axis_index("tm") * rows
    gain = norm_gain[None, :]

    ext = rows + 2 * TILE
    positions = first_row - TILE + jnp.arange(ext, dtype=jnp.int32)
    ends = jnp.cumsum(utt_lengths)
    segment = jnp.sum((ends[:, None] <= positions[None, :]).astype(jnp.int32), axis=0)
    live = lax.dynamic_slice(jnp.pad(pad_mask, TILE), (first_row,), (ext,))
    code = jnp.where(live == 1, segment, -1).reshape(-1, 1, TILE)
    kcode = jnp.concatenate([code[:-1], code[1:]], axis=2)
    qseg = segment[HALO : ext - HALO][:, None]
    live_main = live[TILE : TILE + rows][:, None]
    live_halo = jnp.concatenate(
        [live[TILE - HALO : TILE], live[TILE + rows : TILE + rows + HALO]]
    )[:, None]

    halo_frames, halo_cot = neighbour_rows(frames, cotangent)
    normed_t, masked_t, *main = project(
        frames, gain, qkv_weight, out_weight, cotangent, live_main
    )
    _, _, *halo = project(halo_frames, gain, qkv_weight, out_weight, halo_cot, live_halo)
    return tuple(
        backward(
            qseg, kcode, main, halo, normed_t, masked_t, frames, gain, qkv_weight,
            tm_count, mp_count,
        )
    )


def solution(mesh):
    placed = (
        P(("batch", "tm"), None),
        P(),
        P(None, None, "mp"),
        P("mp", None),
        P(("batch", "tm"), None),
        P("batch"),
        P("batch"),
    )
    return jax.shard_map(
        on_device,
        mesh=mesh,
        in_specs=placed,
        out_specs=(P(("batch", "tm"), "mp"), P("batch", "tm", "mp"), P(("batch", "mp"), "tm")),
        check_vma=False,
    )
```

time: 131 us -> 103 us (0.79)
  waiting for transfers between devices: 35.4 us -> 0.01 us
  Pallas kernels: 60.5 us -> 86.9 us
  between operations: 14.2 us -> 0.75 us
  starting transfers between devices: 6.23 us -> 4.34 us
  local copies, waits for them, and re-layouts: 9.99 us -> 8.2 us
    ppermute x2 -> x0, waiting for transfers between devices: 33.2 us -> none  [the longest x1 33.2 us: on_device(): total = total + lax.ppermute(sums_flat, 'mp', pairs)]
    pallas_call x4 -> x1, Pallas kernels: 46.3 us -> 72.2 us  [backward(): pl.pallas_call(functools.partial(backward_kernel, tm_count, mp_count, gro...]
    ppermute x2 -> x0, starting transfers between devices: 2.49 us -> none  [the longest x1 2.4 us: on_device(): received.append(lax.ppermute(piece, 'mp', pairs))]
    reduce_scatter x1 -> x0, waiting for transfers between devices: 2.2 us -> none  [on_device(): lax.psum_scatter(terms, 'tm', scatter_dimension=0, tiled=True).astype(F32)]
    slice x2 -> x0, local copies, waits for them, and re-layouts: 1.39 us -> none  [on_device(): qkv_grad = summed[:, :3 * cols].reshape(share, 3, cols).transpose(1, 0, 2)]
    dynamic_slice x1 -> x0, local copies, waits for them, and re-layouts: 1.35 us -> none  [on_device(): piece = lax.dynamic_slice_in_dim(dy, target, 1, 0)]
    unnamed x12 -> x11, local copies, waits for them, and re-layouts: 2.99 us -> 3.95 us
  transfers between devices with their start and end apart: 5 -> 2, of which waited for: 2 -> 0; matrix products, arithmetic and copies ran while one was open for 5% -> 4% of each run, Pallas kernels for 18% -> 10%
where the time goes in v2:
time: 103 us
  Pallas kernels  86.9 us (84%)
  local copies, waits for them, and re-layouts  8.2 us (8%)
  starting transfers between devices  4.34 us (4%)
  other arithmetic  2.53 us (2%)
    pallas_call x1, Pallas kernels, backward(): pl.pallas_call(functools.partial(backward_kernel, tm_count, mp_count, gro...  72.2 us
    pallas_call x2, Pallas kernels, project(): pl.pallas_call(project_kernel, name='project', grid=(rows // step,), in_s...  14.6 us
    unnamed x11, local copies, waits for them, and re-layouts  3.95 us
    ppermute x1, starting transfers between devices, neighbour_rows(): low = lax.ppermute(top, 'tm', forward)  3.05 us
  transfers between devices with their start and end apart: 2, of which 0 were waited for; matrix products, arithmetic and copies ran while one was open for 4% of the time, Pallas kernels for 10%

profile of v2, /device:TPU:0, one launch (start us, length us, event | category | flops | bytes accessed | tf_op | source)
XLA Modules:
  0.0 102.7 jit_solution(3122222047882630829)
XLA Ops:
  0.6 0.0 copy-start.3
  0.6 0.0 copy-start.1
  0.7 1.1 %slice_bitcast_fusion.6 = (bf16[1,64,1024]{2,1,0:T(8,128)(2,1)S(1)}, bf16[1,64,1024]{2,1,0:T(8,128)(2,1)S(1)}, bf16[1,64,1024]{2,1,0:T(8,128)(2,1)S(1)}, bf16[1,64,1024]{2,1,0:T(8,128)(2,1)S(1)}) fusion(bf16[1024,1024]{1,0:T(8,128)(2,1)} %cot_ref.1, bf16[1024,1024]{1,0:T(8,128)(2,1)} %x_ref.3), kind=kLoop, calls=%fused_computation.10 | loop fusion | bytes 1048576 | tf_op jit(solution)/shard_map/stack | solution.py:399
  1.8 1.3 %collective-permute-start.1 = (bf16[2,64,1024]{2,1,0:T(8,128)(2,1)S(1)}, bf16[2,64,1024]{2,1,0:T(8,128)(2,1)S(1)}, u32[]{:S(2)}, u32[]{:S(2)}) collective-permute-start(bf16[2,64,1024]{2,1,0:T(8,128)(2,1)S(1)} %pad_maximum_fusion.1), channel_id=1, source_target_pairs={{4,0},{8,4},{12,8},{16,12},{20,16},{24,20},{28,24},{5,1},{9,5},{13... | collective-permute-start | bytes 786440 | tf_op jit(solution)/shard_map/ppermute | solution.py:402
  3.2 3.0 %collective-permute-start = (bf16[2,64,1024]{2,1,0:T(8,128)(2,1)S(1)}, bf16[2,64,1024]{2,1,0:T(8,128)(2,1)S(1)}, u32[]{:S(2)}, u32[]{:S(2)}) collective-permute-start(bf16[2,64,1024]{2,1,0:T(8,128)(2,1)S(1)} %pad_maximum_fusion), channel_id=1, source_target_pairs={{0,4},{4,8},{8,12},{12,16},{16,20},{20,24},{24,28},{1,5},{5,9},{9,... | collective-permute-start | bytes 786440 | tf_op jit(solution)/shard_map/ppermute | solution.py:401
  6.2 0.0 copy-done.3
  6.2 0.2 reduce-window.8
  6.4 0.0 copy-done.1
  6.4 0.1 pad_dynamic-slice_fusion.2
  6.5 0.1 convert_reduce_fusion
  6.6 0.1 fusion.1
  6.7 1.0 copy.14.live_ref
  7.7 10.4 %project.2 = (bf16[1024,1024]{1,0:T(8,128)(2,1)}, bf16[1024,1024]{1,0:T(8,128)(2,1)}, bf16[1024,512]{1,0:T(8,128)(2,1)}, bf16[1024,512]{1,0:T(8,128)(2,1)}, bf16...) custom-call(bf16[1024,1024]{1,0:T(8,128)(2,1)} %x_ref.3, f32[1,1024]{1,0:T(1,128)} %bitcast.23, ...), custom_call_target="tpu_custom_call" | custom-call | flops 4294967296 | bytes 8388608 | tf_op jit(solution)/shard_map/project/pallas_call | solution.py:55
  18.1 0.1 pad_dynamic-slice_fusion.1
  18.2 0.6 pad_add_fusion.kcode_ref
  18.8 0.1 add_bitcast_fusion
  18.9 0.1 slice.80
  18.9 0.8 copy.15.live_ref
  19.7 1.0 %broadcast_in_dim.23.qseg_ref = s32[1152,1]{1,0:T(8,128)} reshape(s32[1152]{0:T(1024)S(1)} %slice.80) | data formatting | bytes 9216 | tf_op jit(solution)/shard_map/broadcast_in_dim | solution.py:420
  20.7 0.0 collective-permute-done.1
  20.8 0.0 collective-permute-done
  20.8 0.7 pad_maximum_fusion.3.cot_ref
  21.5 0.7 pad_maximum_fusion.2.x_ref
  22.2 4.3 %project.3 = (bf16[1024,128]{1,0:T(8,128)(2,1)}, bf16[1024,128]{1,0:T(8,128)(2,1)}, bf16[128,512]{1,0:T(8,128)(2,1)}, bf16[128,512]{1,0:T(8,128)(2,1)}, bf16[128...) custom-call(bf16[128,1024]{1,0:T(8,128)(2,1)} %pad_maximum_fusion.2.x_ref, f32[1,1024]{1,0:T(1,128)} %bitcast.24, ...), custom_call_target="tpu_custom_call" | custom-call | flops 536870912 | bytes 1048576 | tf_op jit(solution)/shard_map/project/pallas_call | solution.py:55
  26.5 72.2 %backward.1 = (bf16[1024,512]{1,0:T(8,128)(2,1)}, f32[3,128,512]{2,1,0:T(8,128)}, f32[512,128]{1,0:T(8,128)}) custom-call(s32[1152,1]{1,0:T(8,128)} %broadcast_in_dim.23.qseg_ref, s32[9,1,256]{2,1,0:T(1,128)} %pad_add_fusion.kcode_ref, bf16[1024,512]{1,0:T(8,128)(2,1)} %get-tuple-element.13.qm, bf16[1024,512]{1,0:T(8,128)(2,1)} %get-tuple-element.14.km, ...), custom_call_target="tpu_custom_call" | custom-call | flops 12884901888 | bytes 31457280 | tf_op jit(solution)/shard_map/backward/pallas_call | solution.py:351
  98.7 0.0 copy-start
  98.7 0.0 copy-start.2
  98.8 2.3 %copy.20 = bf16[1024,512]{1,0:T(8,128)(2,1)} copy(bf16[1024,512]{1,0:T(8,128)(2,1)} %get-tuple-element.40) | data formatting | bytes 2097152
  101.1 0.0 copy-done
  101.1 0.9 copy.21
  102.0 0.0 copy-done.2
  102.0 0.7 copy.22
  (8 shorter events, 0.1 us)
Async XLA Ops:
  0.6 5.6 %copy-start.3 = (s32[8]{0:T(128)S(1)}, s32[8]{0:T(128)}, u32[]{:S(2)}) copy-start(s32[8]{0:T(128)} %param.13) | copy-start | bytes 100
  0.6 5.8 %copy-start.1 = (s32[8192]{0:T(1024)S(1)}, s32[8192]{0:T(1024)}, u32[]{:S(2)}) copy-start(s32[8192]{0:T(1024)} %param.12) | copy-start | bytes 98308
  1.8 18.9 %collective-permute-start.1 = (bf16[2,64,1024]{2,1,0:T(8,128)(2,1)S(1)}, bf16[2,64,1024]{2,1,0:T(8,128)(2,1)S(1)}, u32[]{:S(2)}, u32[]{:S(2)}) collective-permute-start(bf16[2,64,1024]{2,1,0:T(8,128)(2,1)S(1)} %pad_maximum_fusion.1), channel_id=1, source_target_pairs={{4,0},{8,4},{12,8},{16,12},{20,16},{24,20},{28,24},{5,1},{9,5},{13... | collective-permute-start | bytes 786440 | tf_op jit(solution)/shard_map/ppermute | solution.py:402
  3.2 17.6 %collective-permute-start = (bf16[2,64,1024]{2,1,0:T(8,128)(2,1)S(1)}, bf16[2,64,1024]{2,1,0:T(8,128)(2,1)S(1)}, u32[]{:S(2)}, u32[]{:S(2)}) collective-permute-start(bf16[2,64,1024]{2,1,0:T(8,128)(2,1)S(1)} %pad_maximum_fusion), channel_id=1, source_target_pairs={{0,4},{4,8},{8,12},{12,16},{16,20},{20,24},{24,28},{1,5},{5,9},{9,... | collective-permute-start | bytes 786440 | tf_op jit(solution)/shard_map/ppermute | solution.py:401
  98.7 2.4 %copy-start = (f32[3,128,512]{2,1,0:T(8,128)S(1)}, f32[3,128,512]{2,1,0:T(8,128)}, u32[]{:S(2)}) copy-start(f32[3,128,512]{2,1,0:T(8,128)} %get-tuple-element.41) | copy-start | bytes 2359300
  98.7 3.2 %copy-start.2 = (f32[512,128]{1,0:T(8,128)S(1)}, f32[512,128]{1,0:T(8,128)}, u32[]{:S(2)}) copy-start(f32[512,128]{1,0:T(8,128)} %get-tuple-element.42) | copy-start | bytes 786436

commit v3 on v2

--- a/solution.py
+++ b/solution.py
@@ -28,65 +28,20 @@
     )
 
 
-def norm_parts(frames):
-    values = frames.astype(F32)
-    center = values - jnp.mean(values, axis=-1, keepdims=True)
-    inverse = lax.rsqrt(jnp.mean(center * center, axis=-1, keepdims=True) + EPSILON)
-    return center * inverse, inverse
-
-
-def project_kernel(x_ref, gain_ref, w_ref, wo_ref, cot_ref, live_ref,
-                   normed_ref, masked_ref, q_ref, k_ref, v_ref, g_ref):
-    xhat, _ = norm_parts(x_ref[...])
-    normed = (xhat * gain_ref[...]).astype(BF)
-    normed_ref[...] = normed.T
-    for piece, out in enumerate((q_ref, k_ref, v_ref)):
-        out[...] = mm(normed, w_ref[piece], 1, 0).astype(BF)
-    masked = jnp.where(live_ref[...] == 1, cot_ref[...].astype(F32), 0.0).astype(BF)
-    masked_ref[...] = masked.T
-    g_ref[...] = mm(masked, wo_ref[...], 1, 1).astype(BF)
-
-
-def project(frames, gain, w, wo, cot, live):
-    rows, depth = frames.shape
-    cols = w.shape[2]
-    step = min(rows, 256)
-    row = lambda width: pl.BlockSpec((step, width), lambda i: (i, 0))
-    return pl.pallas_call(
-        project_kernel,
-        name="project",
-        grid=(rows // step,),
-        in_specs=[
-            row(depth),
-            pl.BlockSpec((1, depth), lambda i: (0, 0)),
-            pl.BlockSpec(w.shape, lambda i: (0, 0, 0)),
-            pl.BlockSpec(wo.shape, lambda i: (0, 0)),
-            row(depth),
-            row(1),
-        ],
-        out_specs=[pl.BlockSpec((depth, step), lambda i: (0, i))] * 2 + [row(cols)] * 4,
-        out_shape=[jax.ShapeDtypeStruct((depth, rows), BF)] * 2
-        + [jax.ShapeDtypeStruct((rows, cols), BF)] * 4,
-        compiler_params=pltpu.CompilerParams(vmem_limit_bytes=VMEM_LIMIT),
-        cost_estimate=pl.CostEstimate(
-            flops=8 * rows * depth * cols, bytes_accessed=8 * rows * depth, transcendentals=0
-        ),
-    )(frames, gain, w, wo, cot, live)
-
-
 def backward_kernel(tm_count, mp_count, group_cols, block,
-                    qseg_ref, kcode_ref, qm, km, vm, gm, qh, kh, vh, gh,
-                    normed_t, masked_t, x_ref, gain_ref, w_ref,
+                    query_ref, kcode_ref, x_ref, cot_ref, gain_ref, w_ref, wo_ref,
                     frame_ref, qkv_ref, out_ref, *scratch):
     scratch = list(scratch)
+    halo_x, halo_cot, normed_t, masked_t, halo_send, halo_recv = scratch[:6]
+    scratch = scratch[6:]
     qe, ke, ve, ge, oe, dqe, dka, dva, dkb, dvb, stats, centre = scratch[:12]
     own, away, landed, sums_away, sums_landed = scratch[12:17]
     phases = tm_count.bit_length() - 1
     lists = scratch[17 : 17 + phases]
     arrivals = scratch[17 + phases : 17 + 2 * phases]
     (send_sem, recv_sem, share_send, share_recv, sums_send, sums_recv) = scratch[17 + 2 * phases :]
-    rows, cols = qm.shape
-    depth = x_ref.shape[1]
+    rows, depth = x_ref.shape
+    cols = w_ref.shape[2]
     share = depth // mp_count
     chunk = depth // tm_count
     groups = cols // group_cols
@@ -97,21 +52,82 @@
     partners = [tm_at + (1 - 2 * bits[b]) * (1 << b) for b in range(phases)]
     mp_targets = [lax.rem(mp_at + shift, mp_count) for shift in range(1, mp_count)]
 
+    after = lax.rem(tm_at + 1, tm_count)
+    before = lax.rem(tm_at + tm_count - 1, tm_count)
+
     barrier = pltpu.get_barrier_semaphore()
-    for partner in partners:
+    for partner in partners + [after, before]:
         pl.semaphore_signal(barrier, inc=1, device_id={"tm": partner},
                             device_id_type=pl.DeviceIdType.MESH)
     for target in mp_targets:
         pl.semaphore_signal(barrier, inc=1, device_id={"mp": target},
                             device_id_type=pl.DeviceIdType.MESH)
-    pl.semaphore_wait(barrier, phases + mp_count - 1)
-
-    for ext, main, halo in ((qe, qm, qh), (ke, km, kh), (ve, vm, vh), (ge, gm, gh)):
+    pl.semaphore_wait(barrier, phases + mp_count + 1)
+
+    halos = []
+    for source, target in ((x_ref, halo_x), (cot_ref, halo_cot)):
+        for start, slot, device in ((rows - HALO, 0, after), (0, 1, before)):
+            halos.append(
+                pltpu.make_async_remote_copy(
+                    src_ref=source.at[pl.ds(start, HALO)],
+                    dst_ref=target.at[pl.ds(slot * HALO, HALO)],
+                    send_sem=halo_send.at[len(halos)],
+                    recv_sem=halo_recv.at[len(halos)],
+                    device_id={"tm": device},
+                    device_id_type=pl.DeviceIdType.MESH,
+                )
+            )
+    for item in halos:
+        item.start()
+
+    for ext in (qe, ke, ve, ge):
         ext[0 : TILE - HALO] = jnp.zeros((TILE - HALO, cols), BF)
-        ext[TILE - HALO : TILE] = halo[0:HALO]
-        ext[TILE:edge] = main[...]
-        ext[edge : edge + HALO] = halo[HALO : 2 * HALO]
         ext[edge + HALO : edge + TILE] = jnp.zeros((TILE - HALO, cols), BF)
+
+    def project(values, cot, live):
+        mean = jnp.mean(values, axis=-1, keepdims=True)
+        center = values - mean
+        inverse = lax.rsqrt(jnp.mean(center * center, axis=-1, keepdims=True) + EPSILON)
+        normed = (center * inverse * gain_ref[...]).astype(BF)
+        masked = jnp.where(live == 1, cot.astype(F32), 0.0).astype(BF)
+        outs = [mm(normed, w_ref[piece], 1, 0).astype(BF) for piece in range(3)]
+        outs.append(mm(masked, wo_ref[...], 1, 1).astype(BF))
+        return mean, inverse, normed, masked, outs
+
+    def project_rows(i, carry):
+        r = pl.multiple_of(i * block, block)
+        mean, inverse, normed, masked, outs = project(
+            x_ref[pl.ds(r, block), :].astype(F32),
+            cot_ref[pl.ds(r, block), :],
+            query_ref[pl.ds(r + HALO, block), 1:2],
+        )
+        centre[pl.ds(r, block), 0:1] = mean
+        centre[pl.ds(r, block), 1:2] = inverse
+        normed_t[:, pl.ds(r, block)] = normed.T
+        masked_t[:, pl.ds(r, block)] = masked.T
+        for ext, out in zip((qe, ke, ve, ge), outs):
+            ext[pl.ds(r + TILE, block), :] = out
+        return carry
+
+    lax.fori_loop(0, rows // block, project_rows, 0)
+    for item in halos:
+        item.wait_recv()
+    at_row = lax.broadcasted_iota(jnp.int32, (2 * HALO, 1), 0)
+    inside = jnp.where(
+        at_row < HALO,
+        jnp.where(tm_at > 0, 1, 0),
+        jnp.where(tm_at < tm_count - 1, 1, 0),
+    )
+    live = jnp.concatenate(
+        [query_ref[0:HALO, 1:2], query_ref[HALO + rows : 2 * HALO + rows, 1:2]]
+    )
+    outs = project(
+        jnp.where(inside == 1, halo_x[...].astype(F32), 0.0), halo_cot[...], live
+    )[-1]
+    for ext, out in zip((qe, ke, ve, ge), outs):
+        ext[TILE - HALO : TILE] = out[:HALO]
+        ext[edge : edge + HALO] = out[HALO:]
+
     dka[...] = jnp.zeros_like(dka)
     dva[...] = jnp.zeros_like(dva)
     scale = HS ** (-0.5)
@@ -126,7 +142,7 @@
             k0 = pl.multiple_of(t * TILE, TILE)
             q0 = pl.multiple_of(t * TILE + HALO, HALO)
             allowed = band & (
-                diagonal | (qseg_ref[pl.ds(k0, TILE), :] == kcode_ref[t])
+                diagonal | (query_ref[pl.ds(k0, TILE), 0:1] == kcode_ref[t])
             )
             for h in range(group * group_cols // HS, (group + 1) * group_cols // HS):
                 sl = slice(h * HS, (h + 1) * HS)
@@ -209,15 +225,6 @@
                 out_ref[sl, :] = second.T
         progress[unit] = b + 1
 
-    def moments():
-        for r in range(0, rows, block):
-            values = x_ref[r : r + block].astype(F32)
-            mean = jnp.mean(values, axis=-1, keepdims=True)
-            center = values - mean
-            inverse = lax.rsqrt(jnp.mean(center * center, axis=-1, keepdims=True) + EPSILON)
-            centre[r : r + block, 0:1] = mean
-            centre[r : r + block, 1:2] = inverse
-
     def incoming(target, r):
         lane = pl.multiple_of(target * share, 128)
         span = pl.ds(lane, share)
@@ -315,7 +322,6 @@
     if groups == 1:
         attend(0, 0, tiles)
     close(groups - 1)
-    moments()
     away_shares()
     terms(2 * groups - 2)
     terms(2 * groups - 1)
@@ -326,6 +332,8 @@
             if progress[unit] == b:
                 advance(unit)
     norm_rows()
+    for item in halos:
+        item.wait_send()
     for unit in range(2 * groups):
         for b in range(phases):
             copies[unit, b].wait_send()
@@ -333,9 +341,9 @@
         item.wait_send()
 
 
-def backward(qseg, kcode, main, halo, normed_t, masked_t, frames, gain, w, tm_count, mp_count):
-    rows, cols = main[0].shape
-    depth = frames.shape[1]
+def backward(query, kcode, frames, cot, gain, w, wo, tm_count, mp_count):
+    rows, depth = frames.shape
+    cols = w.shape[2]
     ext = rows + 2 * TILE
     share = depth // mp_count
     chunk = depth // tm_count
@@ -351,14 +359,17 @@
     return pl.pallas_call(
         functools.partial(backward_kernel, tm_count, mp_count, group_cols, block),
         name="backward",
-        in_specs=[vmem] * 15,
+        in_specs=[vmem] * 7,
         out_specs=[vmem] * 3,
         out_shape=[
             jax.ShapeDtypeStruct((rows, share), BF),
             jax.ShapeDtypeStruct((3, chunk, cols), F32),
             jax.ShapeDtypeStruct((cols, chunk), F32),
         ],
-        scratch_shapes=[pltpu.VMEM((ext, cols), BF)] * 6
+        scratch_shapes=[pltpu.VMEM((2 * HALO, depth), BF)] * 2
+        + [pltpu.VMEM((depth, rows), BF)] * 2
+        + [dma((4,))] * 2
+        + [pltpu.VMEM((ext, cols), BF)] * 6
         + [pltpu.VMEM((ext, cols), F32)] * 2
         + [pltpu.VMEM((rows, cols), BF)] * 2
         + [pltpu.VMEM((rows, 2), F32)] * 2
@@ -388,19 +399,7 @@
             flops=24 * rows * depth * cols, bytes_accessed=30 * rows * depth,
             transcendentals=rows * cols,
         ),
-    )(qseg, kcode, *main, *halo, normed_t, masked_t, frames, gain, w)
-
-
-def neighbour_rows(frames, cot):
-    count = lax.axis_size("tm")
-    forward = [(i, i + 1) for i in range(count - 1)]
-    backward = [(target, source) for source, target in forward]
-    rows = frames.shape[0]
-    top = jnp.stack([frames[rows - HALO :], cot[rows - HALO :]])
-    bottom = jnp.stack([frames[:HALO], cot[:HALO]])
-    low = lax.ppermute(top, "tm", forward)
-    high = lax.ppermute(bottom, "tm", backward)
-    return jnp.concatenate([low[0], high[0]]), jnp.concatenate([low[1], high[1]])
+    )(query, kcode, frames, cot, gain, w, wo)
 
 
 def on_device(frames, norm_gain, qkv_weight, out_weight, cotangent, pad_mask, utt_lengths):
@@ -417,21 +416,10 @@
     live = lax.dynamic_slice(jnp.pad(pad_mask, TILE), (first_row,), (ext,))
     code = jnp.where(live == 1, segment, -1).reshape(-1, 1, TILE)
     kcode = jnp.concatenate([code[:-1], code[1:]], axis=2)
-    qseg = segment[HALO : ext - HALO][:, None]
-    live_main = live[TILE : TILE + rows][:, None]
-    live_halo = jnp.concatenate(
-        [live[TILE - HALO : TILE], live[TILE + rows : TILE + rows + HALO]]
-    )[:, None]
-
-    halo_frames, halo_cot = neighbour_rows(frames, cotangent)
-    normed_t, masked_t, *main = project(
-        frames, gain, qkv_weight, out_weight, cotangent, live_main
-    )
-    _, _, *halo = project(halo_frames, gain, qkv_weight, out_weight, halo_cot, live_halo)
+    query = jnp.stack([segment, live], axis=1)[HALO : ext - HALO]
     return tuple(
         backward(
-            qseg, kcode, main, halo, normed_t, masked_t, frames, gain, qkv_weight,
-            tm_count, mp_count,
+            query, kcode, frames, cotangent, gain, qkv_weight, out_weight, tm_count, mp_count
         )
     )
 

time: 103 us -> 85.4 us (0.83)
  Pallas kernels: 86.9 us -> 77 us
  starting transfers between devices: 4.34 us -> 0 us
  local copies, waits for them, and re-layouts: 8.2 us -> 5.05 us
    pallas_call x2 -> x0, Pallas kernels: 14.6 us -> none  [project(): pl.pallas_call(project_kernel, name='project', grid=(rows // step,), in_s...]
    pallas_call x1, Pallas kernels: 72.2 us -> 77 us  [backward(): pl.pallas_call(functools.partial(backward_kernel, tm_count, mp_count, gro...]
    ppermute x2 -> x0, starting transfers between devices: 4.34 us -> none  [the longest x1 3.05 us: neighbour_rows(): low = lax.ppermute(top, 'tm', forward)]
    broadcast_in_dim x3 -> x0, local copies, waits for them, and re-layouts: 2.82 us -> none  [the longest x1 1.03 us: on_device(): qseg = segment[HALO:ext - HALO][:, None]]
    concatenate x2 -> x0, other arithmetic: 1.44 us -> none  [the longest x1 0.72 us: neighbour_rows(): jnp.concatenate([low[0], high[0]])]
    another operation x1 -> x2, local copies, waits for them, and re-layouts: 1.14 us -> 0.01 us  [on_device(): query = jnp.stack([segment, live], axis=1)[HALO:ext - HALO]]
    unnamed x11 -> x8, local copies, waits for them, and re-layouts: 3.95 us -> 5.01 us
  transfers between devices with their start and end apart: 2 -> 0, of which waited for: 0 -> 0; matrix products, arithmetic and copies ran while one was open for 4% -> 0% of each run, Pallas kernels for 10% -> 0%
where the time goes in v3:
time: 85.4 us; the launch traced here: 85.2 us
  Pallas kernels  77 us (90%)
  local copies, waits for them, and re-layouts  5.05 us (6%)
  other arithmetic  2.41 us (3%)
    pallas_call x1, Pallas kernels, backward(): pl.pallas_call(functools.partial(backward_kernel, tm_count, mp_count, gro...  77 us
    unnamed x8, local copies, waits for them, and re-layouts  5.01 us

profile of v3, /device:TPU:0, one launch (start us, length us, event | category | flops | bytes accessed | tf_op | source)
XLA Modules:
  0.0 85.2 jit_solution(13373637926066183133)
XLA Ops:
  0.6 0.8 reduce-window.8
  1.5 0.1 convert_reduce_fusion
  1.6 0.8 compare_select_fusion
  2.4 0.1 pad_add_fusion
  2.5 0.6 pad_add_fusion.1.kcode_ref
  3.1 1.1 %copy.14.query_ref = s32[1152,2]{1,0:T(8,128)} copy(s32[1152,2]{0,1:T(2,128)S(1)} %pad_add_fusion) | data formatting | bytes 18432
  4.2 77.0 %backward.1 = (bf16[1024,512]{1,0:T(8,128)(2,1)}, f32[3,128,512]{2,1,0:T(8,128)}, f32[512,128]{1,0:T(8,128)}) custom-call(s32[1152,2]{1,0:T(8,128)} %copy.14.query_ref, s32[9,1,256]{2,1,0:T(1,128)} %pad_add_fusion.1.kcode_ref, bf16[1024,1024]{1,0:T(8,128)(2,1)} %x_ref.1, bf16[1024,1024]{1,0:T(8,128)(2,1)} %cot_ref.1, f32[1,1024]{1,0:T(1,128)} %bitcast.4, ...), custom_call_target="tpu_custom_call" | custom-call | flops 12884901888 | bytes 31457280 | tf_op jit(solution)/shard_map/backward/pallas_call | solution.py:359
  81.2 0.0 copy-start
  81.2 0.0 copy-start.1
  81.2 2.3 %copy.18 = bf16[1024,512]{1,0:T(8,128)(2,1)} copy(bf16[1024,512]{1,0:T(8,128)(2,1)} %get-tuple-element.10) | data formatting | bytes 2097152
  83.6 0.0 copy-done
  83.6 0.9 %copy.19 = f32[3,128,512]{2,1,0:T(8,128)} copy(f32[3,128,512]{2,1,0:T(8,128)S(1)} %copy-done) | data formatting | bytes 1572864
  84.5 0.0 copy-done.1
  84.5 0.7 copy.20
  (6 shorter events, 0.0 us)
Async XLA Ops:
  81.2 2.4 %copy-start = (f32[3,128,512]{2,1,0:T(8,128)S(1)}, f32[3,128,512]{2,1,0:T(8,128)}, u32[]{:S(2)}) copy-start(f32[3,128,512]{2,1,0:T(8,128)} %get-tuple-element.11) | copy-start | bytes 2359300
  81.2 3.2 %copy-start.1 = (f32[512,128]{1,0:T(8,128)S(1)}, f32[512,128]{1,0:T(8,128)}, u32[]{:S(2)}) copy-start(f32[512,128]{1,0:T(8,128)} %get-tuple-element.12) | copy-start | bytes 786436

commit v4 on v3

--- a/solution.py
+++ b/solution.py
@@ -163,7 +163,14 @@
                 dva[pl.ds(k0, 2 * TILE), sl] += mm(pb, g, 0, 0)
             return carry
 
-        lax.fori_loop(lo, hi, tile, 0)
+        def three(i, carry):
+            for j in range(3):
+                tile(lo + 3 * i + j, carry)
+            return carry
+
+        whole = (hi - lo) // 3
+        lax.fori_loop(0, whole, three, 0)
+        lax.fori_loop(lo + 3 * whole, hi, tile, 0)
 
     def close(group):
         sl = slice(group * group_cols, (group + 1) * group_cols)

time: 85.4 us -> 84.9 us (level)
  no operation moved by 1% of the time
where the time goes in v4:
time: 84.9 us; the launch traced here: 84.6 us
  Pallas kernels  76.5 us (90%)
  local copies, waits for them, and re-layouts  5.05 us (6%)
  other arithmetic  2.41 us (3%)
    pallas_call x1, Pallas kernels, backward(): pl.pallas_call(functools.partial(backward_kernel, tm_count, mp_count, gro...  76.5 us
    unnamed x8, local copies, waits for them, and re-layouts  5.01 us

profile of v4, /device:TPU:0, one launch (start us, length us, event | category | flops | bytes accessed | tf_op | source)
XLA Modules:
  0.0 84.6 jit_solution(8618320603282835973)
XLA Ops:
  0.6 0.8 reduce-window.8
  1.5 0.1 convert_reduce_fusion
  1.6 0.8 compare_select_fusion
  2.4 0.1 pad_add_fusion
  2.5 0.6 pad_add_fusion.1.kcode_ref
  3.1 1.1 %copy.14.query_ref = s32[1152,2]{1,0:T(8,128)} copy(s32[1152,2]{0,1:T(2,128)S(1)} %pad_add_fusion) | data formatting | bytes 18432
  4.2 76.5 %backward.1 = (bf16[1024,512]{1,0:T(8,128)(2,1)}, f32[3,128,512]{2,1,0:T(8,128)}, f32[512,128]{1,0:T(8,128)}) custom-call(s32[1152,2]{1,0:T(8,128)} %copy.14.query_ref, s32[9,1,256]{2,1,0:T(1,128)} %pad_add_fusion.1.kcode_ref, bf16[1024,1024]{1,0:T(8,128)(2,1)} %x_ref.1, bf16[1024,1024]{1,0:T(8,128)(2,1)} %cot_ref.1, f32[1,1024]{1,0:T(1,128)} %bitcast.4, ...), custom_call_target="tpu_custom_call" | custom-call | flops 12884901888 | bytes 31457280 | tf_op jit(solution)/shard_map/backward/pallas_call | solution.py:366
  80.7 0.0 copy-start
  80.7 0.0 copy-start.1
  80.7 2.3 %copy.18 = bf16[1024,512]{1,0:T(8,128)(2,1)} copy(bf16[1024,512]{1,0:T(8,128)(2,1)} %get-tuple-element.10) | data formatting | bytes 2097152
  83.0 0.0 copy-done
  83.0 0.9 %copy.19 = f32[3,128,512]{2,1,0:T(8,128)} copy(f32[3,128,512]{2,1,0:T(8,128)S(1)} %copy-done) | data formatting | bytes 1572864
  83.9 0.0 copy-done.1
  83.9 0.7 copy.20
  (6 shorter events, 0.0 us)
Async XLA Ops:
  80.7 2.4 %copy-start = (f32[3,128,512]{2,1,0:T(8,128)S(1)}, f32[3,128,512]{2,1,0:T(8,128)}, u32[]{:S(2)}) copy-start(f32[3,128,512]{2,1,0:T(8,128)} %get-tuple-element.11) | copy-start | bytes 2359300
  80.7 3.2 %copy-start.1 = (f32[512,128]{1,0:T(8,128)S(1)}, f32[512,128]{1,0:T(8,128)}, u32[]{:S(2)}) copy-start(f32[512,128]{1,0:T(8,128)} %get-tuple-element.12) | copy-start | bytes 786436
